TPU v7x, 128 devices: a whole 4x4x4 slice. The times are simulated.
128 devices in a mesh: mem: 4 (over y), brick: 32 (over z, x, core).
Axes of the slice: x: 4, y: 4, z: 4, core: 2. Of those that a mesh axis runs over, the one named last changes fastest.
Arguments:
- members: float32 [128, 524288], P('mem', 'brick'), may hold values from -6 to 6
- predicted: float32 [128, 40, 4096], P('brick', None, 'mem'), may hold values from -6 to 6
- perturbation: float32 [128, 40, 4096], P('brick', None, 'mem'), may hold values from -6 to 6
- observed: float32 [40, 4096], P(None, ('mem', 'brick')), may hold values from -6 to 6
- noise_std: float32 [40, 4096], P(None, ('mem', 'brick')), may hold values from 0.3 to 3
- taper_weights: bfloat16 [4096, 512], P(('mem', 'brick')), may hold values from 0.099609375 to 1
- foot_brick: int32 [4096, 1], P(('mem', 'brick')), may hold values from 0 to 31; in each aligned block of 32 rows (0 to 31, 32 to 63, ...) at most 2 rows name the same one
- foot_tiles: int32 [4096, 4], P(('mem', 'brick')), may hold values from 0 to 127
Outputs:
- updated: float32 [128, 524288], P('mem', 'brick')
Inputs may be any that keep to these rules, and one draw needn't show every extreme that they name: `foot_brick`: among the 32 soundings of one owner (aligned blocks of rows) at most 2 have their footprint in one brick, and some brick receives exactly 2 from some owner in every draw. `foot_tiles`: tile numbers inside the sounding's brick.
All inputs are finite; a program needn't handle non-finite values.
Results may differ from a plain program's by a relative error of at most 0.012.
Values may be sent and summed in bfloat16 or wider, within the bound.
No kernel may reach another device: no remote copies, remote signals or barrier semaphores. Data moves between devices by JAX's collectives and lax.ppermute only.
A program may use at most 64 MiB of HBM per device.

v0:
```python
import jax
import jax.numpy as jnp
from jax import lax
from jax.experimental import pallas as pl
from jax.experimental.pallas import tpu as pltpu
from jax.sharding import PartitionSpec as P

F32 = jnp.float32
BF16 = jnp.bfloat16
VMEM_LIMIT = 56 * 1024 * 1024
LANES = 128


def slot_of(brick_ref, count_ref, s, capacity):
    dest = brick_ref[s]
    rank = jnp.minimum(count_ref[dest], capacity - 1)
    count_ref[dest] = rank + 1
    return dest * capacity + rank


def pack_kernel(brick_ref, pred_ref, pert_ref, out_ref, *, part):
    members, gates, width = pred_ref.shape
    per_tile = LANES // part
    lane = lax.broadcasted_iota(jnp.int32, (gates, LANES), 1) // part
    for which, ref in enumerate((pred_ref, pert_ref)):
        for tile in range(width // LANES):
            blocks = [ref[j, :, tile * LANES : (tile + 1) * LANES] for j in range(members)]
            for q in range(per_tile):
                acc = None
                for j in range(members):
                    shift = ((j - q) * part) % LANES
                    moved = pltpu.roll(blocks[j], shift, 1) if shift else blocks[j]
                    acc = moved if acc is None else jnp.where(lane == j, moved, acc)
                out_ref[tile * per_tile + q, which * gates : (which + 1) * gates, :] = acc.astype(
                    BF16
                )


def taper_kernel(brick_ref, taper_ref, tiles_ref, out_ref, rows_ref, slots_ref, count_ref):
    soundings, length = taper_ref.shape
    pieces = length // LANES
    bricks = out_ref.shape[0] // (out_ref.shape[0] // count_ref.shape[0])
    rows_ref[...] = jnp.zeros_like(rows_ref)
    slots_ref[...] = jnp.zeros_like(slots_ref)
    for f in range(pieces):
        rows_ref[pl.ds(f, soundings, stride=8), :] = taper_ref[
            :, f * LANES : (f + 1) * LANES
        ].astype(F32)
    rows_ref[pl.ds(pieces, soundings, stride=8), :] = tiles_ref[...]
    capacity = slots_ref.shape[0] // bricks

    def clear(i, _):
        count_ref[i] = 0
        return 0

    lax.fori_loop(0, bricks, clear, 0)

    def place(s, _):
        slot = slot_of(brick_ref, count_ref, s, capacity)
        slots_ref[slot] = rows_ref[pl.ds(pl.multiple_of(s * 8, 8), 8), :]
        return 0

    lax.fori_loop(0, soundings, place, 0)
    packed = slots_ref[...].reshape(bricks, 8 * capacity, LANES).astype(BF16)
    for m in range(out_ref.shape[0] // bricks):
        out_ref[m * bricks : (m + 1) * bricks] = packed


def anomaly_kernel(
    brick_ref, got_ref, send_ref, pred_ref, pert_ref, wide_ref, turned_ref, slots_ref, count_ref
):
    sources = got_ref.shape[0]
    rows = got_ref.shape[1]
    gates = rows // 2
    soundings = pred_ref.shape[0]
    per_lane = LANES // soundings
    wide_ref[...] = got_ref[...].reshape(sources * rows, LANES).astype(F32)
    depth = per_lane * LANES
    r = lax.broadcasted_iota(jnp.int32, (depth, depth), 0)
    c = lax.broadcasted_iota(jnp.int32, (depth, depth), 1)
    want = (
        (c // LANES) * sources + ((c % LANES) // per_lane) + (c % per_lane) * LANES
    )
    select = jnp.where(r == want, 1.0, 0.0).astype(BF16)
    lefts = []
    for group in range(rows // per_lane):
        stack = jnp.concatenate(
            [
                wide_ref[pl.ds(group * per_lane + k, sources, stride=rows), :]
                for k in range(per_lane)
            ],
            axis=0,
        )
        turned = stack.T
        lefts.append(
            jnp.concatenate(
                [turned[j * soundings : (j + 1) * soundings, :] for j in range(per_lane)], axis=1
            ).astype(BF16)
        )
    left = jnp.concatenate(lefts, axis=0)
    placed = jnp.dot(left, select, preferred_element_type=F32)
    for group in range(rows // per_lane):
        for k in range(per_lane):
            g = group * per_lane + k
            block = placed[
                group * soundings : (group + 1) * soundings, k * LANES : (k + 1) * LANES
            ]
            if g < gates:
                turned_ref[0, pl.ds(g, soundings, stride=gates), :] = block
            else:
                turned_ref[1, pl.ds(g - gates, soundings, stride=gates), :] = block
    pred = turned_ref[0].reshape(soundings, gates, LANES)
    pred_ref[...] = pred
    pert_ref[...] = turned_ref[1].reshape(soundings, gates, LANES)
    bricks = count_ref.shape[0]
    capacity = slots_ref.shape[0] // bricks
    slots_ref[...] = jnp.zeros_like(slots_ref)

    def clear(i, _):
        count_ref[i] = 0
        return 0

    lax.fori_loop(0, bricks, clear, 0)

    def place(s, _):
        slot = slot_of(brick_ref, count_ref, s, capacity)
        one = pred_ref[s]
        mean = jnp.sum(one, axis=1, keepdims=True) * (1.0 / LANES)
        slots_ref[slot] = one - mean
        return 0

    lax.fori_loop(0, soundings, place, 0, unroll=4)
    packed = slots_ref[...].reshape(bricks, capacity * gates, LANES).astype(BF16)
    for m in range(send_ref.shape[0] // bricks):
        send_ref[m * bricks : (m + 1) * bricks] = packed


def gain_kernel(
    brick_ref, pred_ref, pert_ref, observed_ref, noise_ref, send_ref, slots_ref, count_ref
):
    soundings, gates, ensemble = pred_ref.shape
    bricks = count_ref.shape[0]
    capacity = slots_ref.shape[0] // bricks
    mems = send_ref.shape[0] // bricks
    block = ensemble // mems
    scale = 1.0 / (ensemble - 1.0)
    slots_ref[...] = jnp.zeros_like(slots_ref)

    def clear(i, _):
        count_ref[i] = 0
        return 0

    lax.fori_loop(0, bricks, clear, 0)
    row = lax.broadcasted_iota(jnp.int32, (gates, LANES), 0)
    lane = lax.broadcasted_iota(jnp.int32, (gates, LANES), 1)
    sub = lax.broadcasted_iota(jnp.int32, (gates, 1), 0)
    head = lax.broadcasted_iota(jnp.int32, (1, LANES), 1)
    unit = 8
    for first in range(0, soundings, unit):
        mats = []
        rights = []
        for s in range(first, first + unit):
            pred = pred_ref[s]
            mean = jnp.sum(pred, axis=1, keepdims=True) * (1.0 / ensemble)
            anomaly = pred - mean
            full = jnp.concatenate(
                [anomaly, jnp.zeros((LANES - gates, ensemble), F32)], axis=0
            )
            cov = lax.dot_general(
                anomaly,
                full,
                (((1,), (1,)), ((), ())),
                precision=lax.Precision.HIGHEST,
                preferred_element_type=F32,
            )
            noise = noise_ref[:, s : s + 1]
            mats.append(cov * scale + jnp.where(row == lane, noise * noise, 0.0))
            rights.append(observed_ref[:, s : s + 1] + noise * pert_ref[s] - pred)
        for k in range(gates):
            for u in range(unit):
                w = mats[u]
                inv = 1.0 / w[k : k + 1, k : k + 1]
                top = jnp.where(head == k, 1.0, w[k : k + 1, :]) * inv
                side = jnp.where(sub == k, -1.0, w[:, k : k + 1])
                kept = jnp.where((lane == k) | (row == k), 0.0, w)
                mats[u] = kept - side * top
        for u in range(unit):
            s = first + u
            solved = (
                jnp.dot(
                    mats[u][:, :gates],
                    rights[u],
                    precision=lax.Precision.HIGHEST,
                    preferred_element_type=F32,
                )
                * scale
            )
            slot = slot_of(brick_ref, count_ref, s, capacity)
            slots_ref[slot, 0:gates, :] = solved
    for d in range(bricks):
        stack = slots_ref[d * capacity : (d + 1) * capacity].reshape(LANES, ensemble)
        turned = stack.T.astype(BF16)
        for m in range(mems):
            send_ref[m * bricks + d] = turned[m * block : (m + 1) * block, :]


def update_kernel(
    tiles_ref, model_ref, anomaly_ref, gain_ref, taper_ref, members_ref, out_ref, *, unit
):
    sources, rows, ensemble = anomaly_ref.shape
    capacity = taper_ref.shape[1] // 8
    gates = rows // capacity
    pieces = tiles_ref.shape[0] // (sources * capacity)
    span = LANES // capacity
    out_ref[...] = members_ref[...]

    def turn(i, _):
        work = []
        for u in range(unit):
            src = i * unit + u
            anomalies = anomaly_ref[src]
            gains = gain_ref[src]
            tapers = taper_ref[src].astype(F32)
            for c in range(capacity):
                where = [
                    pl.multiple_of(tiles_ref[(src * capacity + c) * pieces + f] * LANES, LANES)
                    for f in range(pieces)
                ]
                cells = jnp.concatenate(
                    [model_ref[:, pl.ds(at, LANES)] for at in where], axis=1
                )
                field = jnp.dot(
                    anomalies[c * gates : (c + 1) * gates, :], cells, preferred_element_type=F32
                ).astype(BF16)
                rise = jnp.dot(
                    gains[:, c * span : c * span + gates], field, preferred_element_type=F32
                )
                work.append((where, rise, tapers[8 * c : 8 * c + pieces, :]))
        for where, rise, taper in work:
            for f in range(pieces):
                at = pl.ds(where[f], LANES)
                out_ref[:, at] = (
                    out_ref[:, at]
                    + rise[:, f * LANES : (f + 1) * LANES] * taper[f : f + 1, :]
                )
        return 0

    lax.fori_loop(0, sources // unit, turn, 0)


def params():
    return pltpu.CompilerParams(vmem_limit_bytes=VMEM_LIMIT)


def vmem(n):
    return [pl.BlockSpec(memory_space=pltpu.VMEM)] * n


def smem():
    return pl.BlockSpec(memory_space=pltpu.SMEM)


def body(
    members, predicted, perturbation, observed, noise_std, taper_weights, foot_brick, foot_tiles
):
    mems = lax.axis_size("mem")
    bricks = lax.axis_size("brick")
    devices = mems * bricks
    gates = predicted.shape[1]
    soundings = observed.shape[1]
    ensemble = predicted.shape[0] * bricks
    capacity = 2
    slots = bricks * capacity
    pieces = foot_tiles.shape[1]
    brick = foot_brick[:, 0]
    sds = jax.ShapeDtypeStruct

    model_all = lax.all_gather(members.astype(BF16), "mem", axis=0, tiled=True)

    packed = pl.pallas_call(
        lambda *refs: pack_kernel(*refs, part=soundings),
        out_shape=sds((bricks, 2 * gates, LANES), BF16),
        in_specs=[smem()] + vmem(2),
        out_specs=vmem(1)[0],
        compiler_params=params(),
        name="pack",
    )(brick, predicted, perturbation)
    got = lax.all_to_all(packed, "brick", split_axis=0, concat_axis=0, tiled=True)

    tile_rows = jnp.pad(foot_tiles.astype(F32), ((0, 0), (0, LANES - pieces)))
    taper_send = pl.pallas_call(
        taper_kernel,
        out_shape=sds((devices, 8 * capacity, LANES), BF16),
        in_specs=[smem()] + vmem(2),
        out_specs=vmem(1)[0],
        scratch_shapes=[
            pltpu.VMEM((soundings * 8, LANES), F32),
            pltpu.VMEM((slots, 8, LANES), F32),
            pltpu.SMEM((bricks,), jnp.int32),
        ],
        compiler_params=params(),
        name="route_taper",
    )(brick, taper_weights, tile_rows)
    taper_recv = lax.all_to_all(
        taper_send, ("mem", "brick"), split_axis=0, concat_axis=0, tiled=True
    )
    tiles = (
        taper_recv.reshape(devices, capacity, 8, LANES)[:, :, pieces, :pieces]
        .astype(jnp.int32)
        .reshape(devices * capacity * pieces)
    )

    anomaly_send, pred, pert = pl.pallas_call(
        anomaly_kernel,
        out_shape=(
            sds((devices, capacity * gates, LANES), BF16),
            sds((soundings, gates, ensemble), F32),
            sds((soundings, gates, ensemble), F32),
        ),
        in_specs=[smem()] + vmem(1),
        out_specs=tuple(vmem(3)),
        scratch_shapes=[
            pltpu.VMEM((bricks * 2 * gates, LANES), F32),
            pltpu.VMEM((2, soundings * gates, LANES), F32),
            pltpu.VMEM((slots, gates, LANES), F32),
            pltpu.SMEM((bricks,), jnp.int32),
        ],
        compiler_params=params(),
        name="anomaly",
    )(brick, got)
    anomaly_recv = lax.all_to_all(
        anomaly_send, ("mem", "brick"), split_axis=0, concat_axis=0, tiled=True
    )
    gain_send = pl.pallas_call(
        gain_kernel,
        out_shape=sds((devices, ensemble // mems, LANES), BF16),
        in_specs=[smem()] + vmem(4),
        out_specs=vmem(1)[0],
        scratch_shapes=[
            pltpu.VMEM((slots, LANES // capacity, ensemble), F32),
            pltpu.SMEM((bricks,), jnp.int32),
        ],
        compiler_params=params(),
        name="gain",
    )(brick, pred, pert, observed, noise_std)
    gain_recv = lax.all_to_all(
        gain_send, ("mem", "brick"), split_axis=0, concat_axis=0, tiled=True
    )
    return pl.pallas_call(
        lambda *refs: update_kernel(*refs, unit=2),
        out_shape=sds(members.shape, F32),
        in_specs=[smem()] + vmem(5),
        out_specs=vmem(1)[0],
        compiler_params=params(),
        name="update",
    )(tiles, model_all, anomaly_recv, gain_recv, taper_recv, members)


def solution(mesh):
    in_specs = (
        P("mem", "brick"),
        P("brick", None, "mem"),
        P("brick", None, "mem"),
        P(None, ("mem", "brick")),
        P(None, ("mem", "brick")),
        P(("mem", "brick"), None),
        P(("mem", "brick"), None),
        P(("mem", "brick"), None),
    )
    out_specs = P("mem", "brick")
    return jax.shard_map(body, mesh=mesh, in_specs=in_specs, out_specs=out_specs, check_vma=False)
```

profile of v0, /device:TPU:1, one launch (start us, length us, event | category | flops | bytes accessed | tf_op | source)
XLA Modules:
  0.0 200.5 jit_solution(15821580921886350189)
XLA Ops:
  6.5 0.0 all-gather.2.cloned.1.call-start
  6.5 2.7 %convert_element_type.18 = bf16[32,16384]{1,0:T(8,128)(2,1)} convert(f32[32,16384]{1,0:T(8,128)} %refs_5_.1) | non-fusion elementwise | flops 524288 | bytes 3145728 | tf_op jit(solution)/shard_map/convert_element_type | solution.py:278
  9.2 0.0 copy-start.5
  9.2 0.0 all-gather.2.cloned.1.call-update
  9.2 0.0 copy-start.3
  9.2 0.0 copy-start.4
  9.3 2.7 %pack.1 = bf16[32,80,128]{2,1,0:T(8,128)(2,1)} custom-call(s32[32]{0:T(128)} %bitcast.5, f32[4,40,1024]{2,1,0:T(8,128)} %refs_1_.1, f32[4,40,1024]{2,1,0:T(8,128)} %refs_2_.1), custom_call_target="tpu_custom_call" | custom-call | tf_op jit(solution)/shard_map/pack/pallas_call | solution.py:280
  12.0 9.4 %all-to-all-start.1 = ((bf16[32,80,128]{2,1,0:T(8,128)(2,1)}), bf16[32,80,128]{2,1,0:T(8,128)(2,1)S(1)}, u32[]{:S(2)}, u32[]{:S(2)}) async-start(bf16[32,80,128]{2,1,0:T(8,128)(2,1)} %pack.1), calls=%async_computation.1 | async-start | bytes 1310720 | tf_op jit(solution)/shard_map/all_to_all | solution.py:288
  21.4 0.0 copy-done.5
  21.4 0.1 copy.16
  21.5 0.6 pad.4.tiles_ref
  22.1 2.2 %route_taper.1 = bf16[128,16,128]{2,1,0:T(8,128)(2,1)} custom-call(s32[32]{0:T(128)} %bitcast.6, bf16[32,512]{1,0:T(8,128)(2,1)} %taper_ref.1, f32[32,128]{1,0:T(8,128)} %pad.4.tiles_ref), custom_call_target="tpu_custom_call" | custom-call | tf_op jit(solution)/shard_map/route_taper/pallas_call | solution.py:291
  24.3 10.0 %all-to-all-done.1.got_ref = bf16[32,80,128]{2,1,0:T(8,128)(2,1)S(1)} async-done(((bf16[32,80,128]{2,1,0:T(8,128)(2,1)}), bf16[32,80,128]{2,1,0:T(8,128)(2,1)S(1)}, u32[]{:S(2)}, u32[]{:S(2)}) %all-to-all-start.1) | async-done | bytes 655392 | tf_op jit(solution)/shard_map/all_to_all | solution.py:288
  34.3 0.0 copy-start.2
  34.3 5.8 %all-to-all-start = ((bf16[128,16,128]{2,1,0:T(8,128)(2,1)}), bf16[128,16,128]{2,1,0:T(8,128)(2,1)S(1)}, u32[]{:S(2)}, u32[]{:S(2)}) async-start(bf16[128,16,128]{2,1,0:T(8,128)(2,1)} %route_taper.1), calls=%async_computation | async-start | bytes 1048576 | tf_op jit(solution)/shard_map/all_to_all | solution.py:304
  40.2 0.0 copy-done.3
  40.2 0.7 copy.18.observed_ref
  40.9 0.0 copy-done.4
  40.9 0.7 copy.19.noise_ref
  41.5 0.0 copy-done.2
  41.5 5.1 %anomaly.1 = (bf16[128,80,128]{2,1,0:T(8,128)(2,1)}, f32[32,40,128]{2,1,0:T(8,128)}, f32[32,40,128]{2,1,0:T(8,128)}) custom-call(s32[32]{0:T(128)} %bitcast.7, bf16[32,80,128]{2,1,0:T(8,128)(2,1)} %copy-done.2), custom_call_target="tpu_custom_call" | custom-call | tf_op jit(solution)/shard_map/anomaly/pallas_call | solution.py:313
  46.6 20.5 %gain.1 = bf16[128,32,128]{2,1,0:T(8,128)(2,1)} custom-call(s32[32]{0:T(128)} %bitcast.8, f32[32,40,128]{2,1,0:T(8,128)} %get-tuple-element.9.pred_ref, f32[32,40,128]{2,1,0:T(8,128)} %get-tuple-element.10.pert_ref, f32[40,32]{1,0:T(8,128)} %copy.18.observed_ref, f32[40,32]{1,0:T(8,128)} %copy.19.noise_ref), custom_call_target="tpu_custom_call" | custom-call | tf_op jit(solution)/shard_map/gain/pallas_call | solution.py:334
  67.1 0.0 all-to-all-done.refs_4_
  67.2 29.2 %all_to_all.20.refs_3_ = bf16[128,32,128]{2,1,0:T(8,128)(2,1)} all-to-all(bf16[128,32,128]{2,1,0:T(8,128)(2,1)} %gain.1), channel_id=1, replica_groups=mesh['mem'=4,'brick'=32] {'mem','brick'}, dimensions={0} | all-to-all | bytes 2097152 | tf_op jit(solution)/shard_map/all_to_all | solution.py:346
  96.4 4.3 %all-to-all-start.2 = ((bf16[128,80,128]{2,1,0:T(8,128)(2,1)}), bf16[128,80,128]{2,1,0:T(8,128)(2,1)S(1)}, u32[]{:S(2)}, u32[]{:S(2)}) async-start(bf16[128,80,128]{2,1,0:T(8,128)(2,1)} %get-tuple-element.8), calls=%async_computation.2 | async-start | bytes 5242880 | tf_op jit(solution)/shard_map/all_to_all | solution.py:331
  100.7 0.0 copy-done.1
  100.7 0.1 slice.4
  100.9 0.1 copy_convert_fusion
  101.0 0.8 reshape.8.refs_0_
  101.8 35.2 %all-to-all-done.2.refs_2_ = bf16[128,80,128]{2,1,0:T(8,128)(2,1)S(1)} async-done(((bf16[128,80,128]{2,1,0:T(8,128)(2,1)}), bf16[128,80,128]{2,1,0:T(8,128)(2,1)S(1)}, u32[]{:S(2)}, u32[]{:S(2)}) %all-to-all-start.2) | async-done | bytes 2621472 | tf_op jit(solution)/shard_map/all_to_all | solution.py:331
  136.9 1.5 copy-done
  138.5 55.2 %update.1 = f32[32,16384]{1,0:T(8,128)} custom-call(s32[1024]{0:T(1024)} %reshape.8.refs_0_, bf16[128,16384]{1,0:T(8,128)(2,1)} %all-gather.2.cloned.1.call-done.refs_1_, bf16[128,80,128]{2,1,0:T(8,128)(2,1)} %copy-done, bf16[128,32,128]{2,1,0:T(8,128)(2,1)} %all_to_all.20.refs_3_, bf16[128,16,128]{2,1,0:T(8,128)(2,1)} %copy-done.1, f32[32,16384]{1,0:T(8,128)} %refs_5_.1), custom_call_target="tpu_custom_call" | custom-call | tf_op jit(solution)/shard_map/update/pallas_call | solution.py:349
  (4 shorter events, 0.0 us)
Async XLA Ops:
  6.5 130.4 %all-gather.2.cloned.1.call-start = ((), (), s32[]{:S(2)}) async-start(), calls=%async_computation.4 | async-start | bytes 5242880 | tf_op jit(solution)/shard_map/all_gather | solution.py:278
  9.2 12.2 %copy-start.5 = (s32[32,4]{0,1:T(4,128)S(1)}, s32[32,4]{0,1:T(4,128)}, u32[]{:S(2)}) copy-start(s32[32,4]{0,1:T(4,128)} %param.15) | copy-start | bytes 1540
  9.2 31.0 %copy-start.3 = (f32[40,32]{0,1:T(8,128)S(1)}, f32[40,32]{0,1:T(8,128)}, u32[]{:S(2)}) copy-start(f32[40,32]{0,1:T(8,128)} %param.11) | copy-start | bytes 15364
  9.2 31.6 %copy-start.4 = (f32[40,32]{0,1:T(8,128)S(1)}, f32[40,32]{0,1:T(8,128)}, u32[]{:S(2)}) copy-start(f32[40,32]{0,1:T(8,128)} %param.12) | copy-start | bytes 15364
  12.0 22.4 %all-to-all-start.1 = ((bf16[32,80,128]{2,1,0:T(8,128)(2,1)}), bf16[32,80,128]{2,1,0:T(8,128)(2,1)S(1)}, u32[]{:S(2)}, u32[]{:S(2)}) async-start(bf16[32,80,128]{2,1,0:T(8,128)(2,1)} %pack.1), calls=%async_computation.1 | async-start | bytes 1310720 | tf_op jit(solution)/shard_map/all_to_all | solution.py:288
  34.3 7.2 %copy-start.2 = (bf16[32,80,128]{2,1,0:T(8,128)(2,1)}, bf16[32,80,128]{2,1,0:T(8,128)(2,1)S(1)}, u32[]{:S(2)}) copy-start(bf16[32,80,128]{2,1,0:T(8,128)(2,1)S(1)} %all-to-all-done.1.got_ref) | copy-start | bytes 1966084
  34.3 32.8 %all-to-all-start = ((bf16[128,16,128]{2,1,0:T(8,128)(2,1)}), bf16[128,16,128]{2,1,0:T(8,128)(2,1)S(1)}, u32[]{:S(2)}, u32[]{:S(2)}) async-start(bf16[128,16,128]{2,1,0:T(8,128)(2,1)} %route_taper.1), calls=%async_computation | async-start | bytes 1048576 | tf_op jit(solution)/shard_map/all_to_all | solution.py:304
  67.2 33.6 %copy-start.1 = (bf16[128,16,128]{2,1,0:T(8,128)(2,1)}, bf16[128,16,128]{2,1,0:T(8,128)(2,1)S(1)}, u32[]{:S(2)}) copy-start(bf16[128,16,128]{2,1,0:T(8,128)(2,1)S(1)} %all-to-all-done.refs_4_) | copy-start | bytes 1572868
  96.4 40.5 %all-to-all-start.2 = ((bf16[128,80,128]{2,1,0:T(8,128)(2,1)}), bf16[128,80,128]{2,1,0:T(8,128)(2,1)S(1)}, u32[]{:S(2)}, u32[]{:S(2)}) async-start(bf16[128,80,128]{2,1,0:T(8,128)(2,1)} %get-tuple-element.8), calls=%async_computation.2 | async-start | bytes 5242880 | tf_op jit(solution)/shard_map/all_to_all | solution.py:331
  136.9 1.5 copy-start
Sparse Core Ops, SparseCore 0:
  9.3 57.1 all-gather.1
where the time goes:
time: 201 us
  Pallas kernels  85.7 us (43%)
  waiting for transfers between devices  45.2 us (22%)
  blocking collectives  29.2 us (15%)
  starting transfers between devices  19.6 us (10%)
  between operations  13.5 us (7%)
  local copies, waits for them, and re-layouts  4.51 us (2%)
  other arithmetic  2.75 us (1%)
    pallas_call x1, Pallas kernels, body(): pl.pallas_call(lambda *refs: update_kernel(*refs, unit=2), out_shape=sds(...  55.2 us
    all_to_all x1, waiting for transfers between devices, body(): lax.all_to_all(anomaly_send, ('mem', 'brick'), split_axis=0, concat_axis=...  35.2 us
    all_to_all x1, blocking collectives, body(): lax.all_to_all(gain_send, ('mem', 'brick'), split_axis=0, concat_axis=0,...  29.2 us
    pallas_call x1, Pallas kernels, body(): pl.pallas_call(gain_kernel, out_shape=sds((devices, ensemble // mems, LAN...  20.5 us
    all_to_all x1, waiting for transfers between devices, body(): lax.all_to_all(packed, 'brick', split_axis=0, concat_axis=0, tiled=True)  10 us
    all_to_all x1, starting transfers between devices, body(): lax.all_to_all(packed, 'brick', split_axis=0, concat_axis=0, tiled=True)  9.44 us
    all_to_all x1, starting transfers between devices, body(): lax.all_to_all(taper_send, ('mem', 'brick'), split_axis=0, concat_axis=0,...  5.84 us
    pallas_call x1, Pallas kernels, body(): pl.pallas_call(anomaly_kernel, out_shape=(sds((devices, capacity * gates,...  5.06 us
  transfers between devices with their start and end apart: 4, of which 2 were waited for; matrix products, arithmetic and copies ran while one was open for 2% of the time, Pallas kernels for 15%

commit v1 on v0

v1 whole, which is shorter than its diff:
```python
import jax
import jax.numpy as jnp
from jax import lax
from jax.experimental import pallas as pl
from jax.experimental.pallas import tpu as pltpu
from jax.sharding import PartitionSpec as P

F32 = jnp.float32
BF16 = jnp.bfloat16
VMEM_LIMIT = 56 * 1024 * 1024
LANES = 128


def slot_of(brick_ref, count_ref, s, capacity):
    dest = brick_ref[s]
    rank = jnp.minimum(count_ref[dest], capacity - 1)
    count_ref[dest] = rank + 1
    return dest * capacity + rank


def clear_counts(count_ref):
    def clear(i, _):
        count_ref[i] = 0
        return 0

    lax.fori_loop(0, count_ref.shape[0], clear, 0)


def pack_kernel(pred_ref, pert_ref, out_ref, *, part):
    members, gates, width = pred_ref.shape
    per_tile = LANES // part
    lane = lax.broadcasted_iota(jnp.int32, (gates, LANES), 1) // part
    for which, ref in enumerate((pred_ref, pert_ref)):
        for tile in range(width // LANES):
            blocks = [ref[j, :, tile * LANES : (tile + 1) * LANES] for j in range(members)]
            for q in range(per_tile):
                acc = None
                for j in range(members):
                    shift = ((j - q) * part) % LANES
                    moved = pltpu.roll(blocks[j], shift, 1) if shift else blocks[j]
                    acc = moved if acc is None else jnp.where(lane == j, moved, acc)
                out_ref[tile * per_tile + q, which * gates : (which + 1) * gates, :] = acc.astype(
                    BF16
                )


def taper_kernel(brick_ref, taper_ref, tiles_ref, out_ref, rows_ref, slots_ref, count_ref):
    soundings, length = taper_ref.shape
    bricks = out_ref.shape[0]
    pieces = length // LANES
    rows_ref[...] = jnp.zeros_like(rows_ref)
    slots_ref[...] = jnp.zeros_like(slots_ref)
    for f in range(pieces):
        rows_ref[pl.ds(f, soundings, stride=8), :] = taper_ref[
            :, f * LANES : (f + 1) * LANES
        ].astype(F32)
    numbers = jnp.concatenate(
        [tiles_ref[...].astype(F32), jnp.zeros((LANES - pieces, soundings), F32)], axis=0
    )
    rows_ref[pl.ds(pieces, soundings, stride=8), :] = numbers.T
    capacity = slots_ref.shape[0] // bricks
    clear_counts(count_ref)

    def place(s, _):
        slot = slot_of(brick_ref, count_ref, s, capacity)
        slots_ref[slot] = rows_ref[pl.ds(pl.multiple_of(s * 8, 8), 8), :]
        return 0

    lax.fori_loop(0, soundings, place, 0)
    out_ref[...] = slots_ref[...].reshape(bricks, 8 * capacity, LANES).astype(BF16)


def owner_kernel(
    brick_ref, got_ref, observed_ref, noise_ref, taper_ref, send_ref, wide_ref, turned_ref, count_ref
):
    sources = got_ref.shape[0]
    soundings, gates = observed_ref.shape
    seen_all = observed_ref[...].T
    noise_all = noise_ref[...].T
    rows = 2 * gates
    per_lane = LANES // soundings
    bricks = count_ref.shape[0]
    mems = send_ref.shape[0] // bricks
    block = LANES // mems
    capacity = taper_ref.shape[1] // 8
    filled = capacity * block
    scale = 1.0 / (LANES - 1.0)
    send_ref[:, :filled, :] = jnp.zeros((mems * bricks, filled, LANES), BF16)
    for m in range(mems):
        send_ref[m * bricks : (m + 1) * bricks, filled:, :] = taper_ref[...]
    clear_counts(count_ref)
    wide_ref[...] = got_ref[...].reshape(sources * rows, LANES).astype(F32)
    depth = per_lane * LANES
    r = lax.broadcasted_iota(jnp.int32, (depth, depth), 0)
    c = lax.broadcasted_iota(jnp.int32, (depth, depth), 1)
    want = (c // LANES) * sources + ((c % LANES) // per_lane) + (c % per_lane) * LANES
    select = jnp.where(r == want, 1.0, 0.0).astype(BF16)
    lefts = []
    for group in range(rows // per_lane):
        stack = jnp.concatenate(
            [
                wide_ref[pl.ds(group * per_lane + k, sources, stride=rows), :]
                for k in range(per_lane)
            ],
            axis=0,
        )
        turned = stack.T
        lefts.append(
            jnp.concatenate(
                [turned[j * soundings : (j + 1) * soundings, :] for j in range(per_lane)], axis=1
            ).astype(BF16)
        )
    left = jnp.concatenate(lefts, axis=0)
    placed = jnp.dot(left, select, preferred_element_type=F32)
    for group in range(rows // per_lane):
        for k in range(per_lane):
            g = group * per_lane + k
            turned_ref[g // gates, pl.ds(g % gates, soundings, stride=gates), :] = placed[
                group * soundings : (group + 1) * soundings, k * LANES : (k + 1) * LANES
            ]
    many = LANES // gates
    count = -(-soundings // many)
    sub8 = lax.broadcasted_iota(jnp.int32, (8, LANES), 0)
    lane8 = lax.broadcasted_iota(jnp.int32, (8, LANES), 1)
    base8 = jnp.minimum(lane8 // gates, many - 1) * gates
    within8 = lane8 - base8
    row = lax.broadcasted_iota(jnp.int32, (gates, LANES), 0)
    lane = lax.broadcasted_iota(jnp.int32, (gates, LANES), 1)
    part = lane // gates
    full = lambda x: jnp.concatenate([x, jnp.zeros((LANES - x.shape[0], LANES), F32)], axis=0)
    anomalies, rights, mats = [], [], []
    for t in range(count):
        here = range(t * many, min(soundings, (t + 1) * many))
        span = slice(t * many * gates, t * many * gates + len(here) * gates)
        pred = turned_ref[0, span, :]
        pert = turned_ref[1, span, :]
        anomaly = full(pred - jnp.sum(pred, axis=1, keepdims=True) * (1.0 / LANES))
        noise = jnp.concatenate([noise_all[:, s : s + 1] for s in here], axis=0)
        observed = jnp.concatenate([seen_all[:, s : s + 1] for s in here], axis=0)
        rights.append(full(observed + noise * pert - pred))
        cov = lax.dot_general(
            anomaly,
            anomaly,
            (((1,), (1,)), ((), ())),
            precision=lax.Precision.HIGHEST,
            preferred_element_type=F32,
        )
        mat = jnp.zeros((gates, LANES), F32)
        for u in range(many):
            at = slice(u * gates, (u + 1) * gates)
            if u < len(here):
                variance = noise[at] * noise[at]
                mine = cov[at] * scale + jnp.where(row + u * gates == lane, variance, 0.0)
            else:
                mine = jnp.where(row + u * gates == lane, 1.0, 0.0)
            mat = jnp.where(part == u, mine, mat)
        anomalies.append(anomaly)
        mats.append([mat[8 * i : 8 * i + 8] for i in range(gates // 8)])
    for k in range(gates):
        index = base8 + k
        at_k = within8 == k
        home, line = divmod(k, 8)
        for t in range(count):
            tiles = mats[t]
            sides = [jnp.take_along_axis(x, index, axis=1) for x in tiles]
            top = jnp.where(at_k, 1.0, tiles[home])[line : line + 1] / sides[home][line : line + 1]
            top = jnp.broadcast_to(top, (8, LANES))
            mats[t] = [
                jnp.where(at_k, 0.0, x) - side * top if i != home
                else jnp.where(sub8 == line, top, jnp.where(at_k, 0.0, x) - side * top)
                for i, (x, side) in enumerate(zip(tiles, sides))
            ]
    for t in range(count):
        here = range(t * many, min(soundings, (t + 1) * many))
        inverse = jnp.concatenate(mats[t], axis=0)
        spread = full(
            jnp.concatenate([jnp.where(part == u, inverse, 0.0) for u in range(many)], axis=0)
        )
        solved = (
            jnp.dot(
                spread, rights[t], precision=lax.Precision.HIGHEST, preferred_element_type=F32
            )
            * scale
        )
        gain = solved.T.astype(BF16)
        rounded = anomalies[t].astype(BF16)
        which = lax.broadcasted_iota(jnp.int32, (LANES, LANES), 0) // gates
        right = jnp.concatenate(
            [jnp.where(which == u, rounded, jnp.zeros_like(rounded)) for u in range(len(here))], axis=1
        )
        weight = jnp.dot(gain, right, preferred_element_type=F32).astype(BF16)
        for u, s in enumerate(here):
            slot = slot_of(brick_ref, count_ref, s, capacity)
            first = pl.multiple_of((slot % capacity) * block, block)
            for m in range(mems):
                send_ref[m * bricks + slot // capacity, pl.ds(first, block), :] = weight[
                    m * block : (m + 1) * block, u * LANES : (u + 1) * LANES
                ]


def update_kernel(me_ref, *refs, unit, capacity, pieces):
    parts = refs[:-9]
    recv_ref, members_ref, out_ref, model_ref, taper_ref, turn_ref, tiles_ref, sems, last = refs[-9:]
    ensemble = model_ref.shape[0]
    block = members_ref.shape[0]
    mems = ensemble // block
    half = block // 2
    sources = recv_ref.shape[0]
    filled = capacity * block
    me = me_ref[0]
    spots = [(0, 0, block), (1, 0, block), (3, 0, block), (2, 0, half), (2, half, half)]
    copies = [pltpu.make_async_copy(members_ref, out_ref, sems.at[len(spots)])]
    for n, (ref, (r, start, size)) in enumerate(zip(parts, spots)):
        first = pl.multiple_of(((me - r) & (mems - 1)) * block + start, half)
        copies.append(pltpu.make_async_copy(ref, model_ref.at[pl.ds(first, size), :], sems.at[n]))
    for copy in copies:
        copy.start()
    taper_ref[...] = recv_ref[:, filled:, :].astype(F32).reshape(sources * 8 * capacity, LANES)
    for c in range(capacity):
        numbers = taper_ref[pl.ds(8 * c + pieces, sources, stride=8 * capacity), :].T
        turn_ref[c] = numbers[:8, :].astype(jnp.int32)
    table = pltpu.make_async_copy(turn_ref, tiles_ref, last)
    table.start()
    table.wait()
    for copy in copies:
        copy.wait()

    def turn(i, _):
        items = []
        for u in range(unit):
            src = i * unit + u
            for c in range(capacity):
                where = [
                    pl.multiple_of(tiles_ref[c, f, src] * LANES, LANES) for f in range(pieces)
                ]
                items.append((src, c, where))
        rises = []
        for src, c, where in items:
            cells = jnp.concatenate([model_ref[:, pl.ds(at, LANES)] for at in where], axis=1)
            weight = recv_ref[src, c * block : (c + 1) * block, :]
            rises.append(jnp.dot(weight, cells, preferred_element_type=F32))
        for (src, c, where), rise in zip(items, rises):
            rows = pl.multiple_of((src * capacity + c) * 8, 8)
            taper = taper_ref[pl.ds(rows, 8), :]
            for f in range(pieces):
                at = pl.ds(where[f], LANES)
                out_ref[:, at] = (
                    out_ref[:, at] + rise[:, f * LANES : (f + 1) * LANES] * taper[f : f + 1, :]
                )
        return 0

    lax.fori_loop(0, sources // unit, turn, 0)


def params():
    return pltpu.CompilerParams(vmem_limit_bytes=VMEM_LIMIT)


def cost(us):
    return pl.CostEstimate(flops=us * 1000000000, transcendentals=0, bytes_accessed=us * 3000000)


def vmem(n):
    return [pl.BlockSpec(memory_space=pltpu.VMEM)] * n


def smem():
    return pl.BlockSpec(memory_space=pltpu.SMEM)


def body(
    members, predicted, perturbation, observed, noise_std, taper_weights, foot_brick, foot_tiles
):
    mems = lax.axis_size("mem")
    bricks = lax.axis_size("brick")
    devices = mems * bricks
    gates = predicted.shape[1]
    soundings = observed.shape[1]
    ensemble = predicted.shape[0] * bricks
    capacity = 2
    slots = bricks * capacity
    pieces = foot_tiles.shape[1]
    brick = foot_brick[:, 0]
    sds = jax.ShapeDtypeStruct

    def shifted(x, by):
        return lax.ppermute(x, "mem", [(i, (i + by) % mems) for i in range(mems)])

    packed = pl.pallas_call(
        lambda *refs: pack_kernel(*refs, part=soundings),
        out_shape=sds((bricks, 2 * gates, LANES), BF16),
        in_specs=vmem(2),
        out_specs=vmem(1)[0],
        compiler_params=params(),
        cost_estimate=cost(3),
        name="pack",
    )(predicted, perturbation)
    got = lax.all_to_all(packed, "brick", split_axis=0, concat_axis=0, tiled=True)

    held, _ = lax.optimization_barrier((members, packed))
    model0 = held.astype(BF16)
    model1, model3 = shifted(model0, 1), shifted(model0, -1)

    brick, _ = lax.optimization_barrier((brick, packed))
    taper_rows = pl.pallas_call(
        taper_kernel,
        out_shape=sds((bricks, 8 * capacity, LANES), BF16),
        in_specs=[smem()] + vmem(2),
        out_specs=vmem(1)[0],
        scratch_shapes=[
            pltpu.VMEM((soundings * 8, LANES), F32),
            pltpu.VMEM((slots, 8, LANES), F32),
            pltpu.SMEM((bricks,), jnp.int32),
        ],
        compiler_params=params(),
        cost_estimate=cost(2),
        name="route_taper",
    )(brick, taper_weights, foot_tiles.T)

    weight_send = pl.pallas_call(
        owner_kernel,
        out_shape=sds((devices, capacity * (ensemble // mems + 8), ensemble), BF16),
        in_specs=[smem()] + vmem(4),
        out_specs=vmem(1)[0],
        scratch_shapes=[
            pltpu.VMEM((bricks * 2 * gates, LANES), F32),
            pltpu.VMEM((2, soundings * gates, LANES), F32),
            pltpu.SMEM((bricks,), jnp.int32),
        ],
        compiler_params=params(),
        cost_estimate=cost(15),
        name="owner",
    )(brick, got, observed.T, noise_std.T, taper_rows)
    weight_send, model1, model3 = lax.optimization_barrier((weight_send, model1, model3))
    half = members.shape[0] // 2
    upper2, lower2 = shifted(model1[:half], 1), shifted(model3[half:], -1)
    blocks = (model0, model1, model3, upper2, lower2)
    weight_recv = lax.all_to_all(
        weight_send, ("mem", "brick"), split_axis=0, concat_axis=0, tiled=True
    )
    me = lax.axis_index("mem").astype(jnp.int32).reshape(1)
    hbm = pl.BlockSpec(memory_space=pl.ANY)
    weight_recv = pltpu.with_memory_space_constraint(weight_recv, pltpu.VMEM)
    return pl.pallas_call(
        lambda *refs: update_kernel(*refs, unit=16, capacity=capacity, pieces=pieces),
        out_shape=sds(members.shape, F32),
        in_specs=[smem()] + [hbm] * len(blocks) + vmem(1) + [hbm],
        out_specs=vmem(1)[0],
        scratch_shapes=[
            pltpu.VMEM((ensemble, members.shape[1]), BF16),
            pltpu.VMEM((devices * 8 * capacity, LANES), F32),
            pltpu.VMEM((capacity, 8, devices), jnp.int32),
            pltpu.SMEM((capacity, 8, devices), jnp.int32),
            pltpu.SemaphoreType.DMA((len(blocks) + 1,)),
            pltpu.SemaphoreType.DMA(()),
        ],
        compiler_params=params(),
        cost_estimate=cost(20),
        name="update",
    )(me, *blocks, weight_recv, members)


def solution(mesh):
    in_specs = (
        P("mem", "brick"),
        P("brick", None, "mem"),
        P("brick", None, "mem"),
        P(None, ("mem", "brick")),
        P(None, ("mem", "brick")),
        P(("mem", "brick"), None),
        P(("mem", "brick"), None),
        P(("mem", "brick"), None),
    )
    out_specs = P("mem", "brick")
    return jax.shard_map(body, mesh=mesh, in_specs=in_specs, out_specs=out_specs, check_vma=False)
```

time: 201 us -> 108 us (0.54)
  Pallas kernels: 85.7 us -> 36.2 us
  blocking collectives: 29.2 us -> 0 us
  between operations: 13.5 us -> 0.05 us
  starting transfers between devices: 19.6 us -> 23 us
  other arithmetic: 2.75 us -> 0.1 us
    pallas_call x4 -> x3, Pallas kernels: 83 us -> 33.3 us  [the longest x1 16.4 us: body(): pl.pallas_call(lambda *refs: update_kernel(*refs, unit=16, capacity=capac...]
    ppermute x0 -> x4, waiting for transfers between devices: none -> 37.1 us  [shifted(): return lax.ppermute(x, 'mem', [(i, (i + by) % mems) for i in range(mems)])]
    all_to_all x2 -> x1, waiting for transfers between devices: 35.2 us -> 0.01 us  [body(): lax.all_to_all(weight_send, ('mem', 'brick'), split_axis=0, concat_axis=0...]
    all_to_all x1 -> x0, blocking collectives: 29.2 us -> none  [body(): lax.all_to_all(gain_send, ('mem', 'brick'), split_axis=0, concat_axis=0,...]
    ppermute x0 -> x4, starting transfers between devices: none -> 5.46 us  [shifted(): return lax.ppermute(x, 'mem', [(i, (i + by) % mems) for i in range(mems)])]
    slice x1 -> x2, local copies, waits for them, and re-layouts: 0.14 us -> 2.95 us  [body(): upper2, lower2 = (shifted(model1[:half], 1), shifted(model3[half:], -1))]
    convert_element_type x3 -> x1, other arithmetic: 2.75 us -> 0.1 us  [body(): model0 = held.astype(BF16)]
    unnamed x14 -> x6, local copies, waits for them, and re-layouts: 2.89 us -> 0.47 us
  transfers between devices with their start and end apart: 4 -> 6, of which waited for: 2 -> 4; matrix products, arithmetic and copies ran while one was open for 2% -> 3% of each run, Pallas kernels for 15% -> 16%
where the time goes in v1:
time: 108 us
  waiting for transfers between devices  45.1 us (42%)
  Pallas kernels  36.2 us (34%)
  starting transfers between devices  23 us (21%)
  local copies, waits for them, and re-layouts  3.42 us (3%)
    ppermute x4, waiting for transfers between devices, shifted(): return lax.ppermute(x, 'mem', [(i, (i + by) % mems) for i in range(mems)])  37.1 us
    pallas_call x1, Pallas kernels, body(): pl.pallas_call(lambda *refs: update_kernel(*refs, unit=16, capacity=capac...  16.4 us
    pallas_call x1, Pallas kernels, body(): pl.pallas_call(owner_kernel, out_shape=sds((devices, capacity * (ensemble...  14.9 us
    all_to_all x1, starting transfers between devices, body(): lax.all_to_all(packed, 'brick', split_axis=0, concat_axis=0, tiled=True)  9.48 us
    all_to_all x1, starting transfers between devices, body(): lax.all_to_all(weight_send, ('mem', 'brick'), split_axis=0, concat_axis=0...  8.06 us
    all_to_all x1, waiting for transfers between devices, body(): lax.all_to_all(packed, 'brick', split_axis=0, concat_axis=0, tiled=True)  8.01 us
    ppermute x4, starting transfers between devices, shifted(): return lax.ppermute(x, 'mem', [(i, (i + by) % mems) for i in range(mems)])  5.46 us
    slice x2, local copies, waits for them, and re-layouts, body(): upper2, lower2 = (shifted(model1[:half], 1), shifted(model3[half:], -1))  2.95 us
  transfers between devices with their start and end apart: 6, of which 4 were waited for; matrix products, arithmetic and copies ran while one was open for 3% of the time, Pallas kernels for 16%

profile of v1, /device:TPU:1, one launch (start us, length us, event | category | flops | bytes accessed | tf_op | source)
XLA Modules:
  0.0 107.9 jit_solution(16463954273678221146)
XLA Ops:
  0.0 0.0 copy-start
  0.0 2.8 %pack.1 = bf16[32,80,128]{2,1,0:T(8,128)(2,1)} custom-call(f32[4,40,1024]{2,1,0:T(8,128)} %refs_0_.1, f32[4,40,1024]{2,1,0:T(8,128)} %refs_1_.1), custom_call_target="tpu_custom_call" | custom-call | flops 3000000000 | bytes 9000000 | tf_op jit(solution)/shard_map/pack/pallas_call | solution.py:289
  2.8 9.5 %all-to-all-start = ((bf16[32,80,128]{2,1,0:T(8,128)(2,1)}), bf16[32,80,128]{2,1,0:T(8,128)(2,1)}, u32[]{:S(2)}, u32[]{:S(2)}) async-start(bf16[32,80,128]{2,1,0:T(8,128)(2,1)} %pack.1), calls=%async_computation | async-start | bytes 1310720 | tf_op jit(solution)/shard_map/all_to_all | solution.py:298
  12.3 0.0 copy-done
  12.3 0.1 convert_element_type.3.refs_1_
  12.5 0.0 copy-start.1
  12.5 2.8 %collective-permute-start.1 = (bf16[32,16384]{1,0:T(8,128)(2,1)S(1)}, bf16[32,16384]{1,0:T(8,128)(2,1)S(1)}, u32[]{:S(2)}, u32[]{:S(2)}) collective-permute-start(bf16[32,16384]{1,0:T(8,128)(2,1)S(1)} %convert_element_type.3.refs_1_), channel_id=1, source_target_pairs={{0,96},{32,0},{64,32},{96,64},{1,97},{33,1},{65,33},{97,65},{2,98}... | collective-permute-start | bytes 3145736 | tf_op jit(solution)/shard_map/ppermute | solution.py:287
  15.3 0.0 collective-permute-start
  15.3 2.0 %route_taper.1.taper_ref = bf16[32,16,128]{2,1,0:T(8,128)(2,1)} custom-call(s32[32]{0:T(128)} %bitcast.8, bf16[32,512]{1,0:T(8,128)(2,1)} %taper_ref.1, s32[4,32]{1,0:T(4,128)} %bitcast.7), custom_call_target="tpu_custom_call" | custom-call | flops 2000000000 | bytes 6000000 | tf_op jit(solution)/shard_map/route_taper/pallas_call | solution.py:305
  17.3 0.0 copy-done.1
  17.3 8.0 %all-to-all-done.got_ref = bf16[32,80,128]{2,1,0:T(8,128)(2,1)} async-done(((bf16[32,80,128]{2,1,0:T(8,128)(2,1)}), bf16[32,80,128]{2,1,0:T(8,128)(2,1)}, u32[]{:S(2)}, u32[]{:S(2)}) %all-to-all-start) | async-done | bytes 655392 | tf_op jit(solution)/shard_map/all_to_all | solution.py:298
  25.3 14.9 %owner.1 = bf16[128,80,128]{2,1,0:T(8,128)(2,1)} custom-call(s32[32]{0:T(128)} %bitcast.9, bf16[32,80,128]{2,1,0:T(8,128)(2,1)} %all-to-all-done.got_ref, f32[32,40]{1,0:T(8,128)} %bitcast.5, f32[32,40]{1,0:T(8,128)} %bitcast.6, bf16[32,16,128]{2,1,0:T(8,128)(2,1)} %route_taper.1.taper_ref), custom_call_target="tpu_custom_call" | custom-call | flops 15000000512 | bytes 45000000 | tf_op jit(solution)/shard_map/owner/pallas_call | solution.py:320
  40.2 0.0 collective-permute-done.1.refs_3_
  40.2 0.0 copy-start.2
  40.2 0.5 collective-permute-done.refs_2_
  40.7 0.5 copy-done.2
  41.2 8.1 %all-to-all-start.1 = ((bf16[128,80,128]{2,1,0:T(8,128)(2,1)}), bf16[128,80,128]{2,1,0:T(8,128)(2,1)S(1)}, u32[]{:S(2)}, u32[]{:S(2)}) async-start(bf16[128,80,128]{2,1,0:T(8,128)(2,1)} %owner.1), calls=%async_computation.1 | async-start | bytes 5242880 | tf_op jit(solution)/shard_map/all_to_all | solution.py:338
  49.3 1.1 slice.6
  50.3 1.9 %slice.7 = bf16[16,16384]{1,0:T(8,128)(2,1)} slice(bf16[32,16384]{1,0:T(8,128)(2,1)} %copy-done.2), slice={[16:32], [0:16384]} | slice | bytes 1048576 | tf_op jit(solution)/shard_map/slice | solution.py:336
  52.2 2.6 %collective-permute-start.3 = (bf16[16,16384]{1,0:T(8,128)(2,1)}, bf16[16,16384]{1,0:T(8,128)(2,1)}, u32[]{:S(2)}, u32[]{:S(2)}) collective-permute-start(bf16[16,16384]{1,0:T(8,128)(2,1)} %slice.7), channel_id=1, source_target_pairs={{0,96},{32,0},{64,32},{96,64},{1,97},{33,1},{65,33},{97,65},{2,98}... | collective-permute-start | bytes 1572872 | tf_op jit(solution)/shard_map/ppermute | solution.py:287
  54.9 0.0 collective-permute-start.2
  54.9 35.3 %collective-permute-done.3.refs_5_ = bf16[16,16384]{1,0:T(8,128)(2,1)} collective-permute-done((bf16[16,16384]{1,0:T(8,128)(2,1)}, bf16[16,16384]{1,0:T(8,128)(2,1)}, u32[]{:S(2)}, u32[]{:S(2)}) %collective-permute-start.3) | collective-permute-done | bytes 524320 | tf_op jit(solution)/shard_map/ppermute | solution.py:287
  90.2 1.3 %collective-permute-done.2.refs_4_ = bf16[16,16384]{1,0:T(8,128)(2,1)} collective-permute-done((bf16[16,16384]{1,0:T(8,128)(2,1)S(1)}, bf16[16,16384]{1,0:T(8,128)(2,1)}, u32[]{:S(2)}, u32[]{:S(2)}) %collective-permute-start.2) | collective-permute-done | bytes 524320 | tf_op jit(solution)/shard_map/ppermute | solution.py:287
  91.4 0.0 all-to-all-done.1.refs_6_
  91.4 16.4 %update.1 = f32[32,16384]{1,0:T(8,128)} custom-call(s32[1]{0:T(128)} %bitcast.refs_0_, bf16[32,16384]{1,0:T(8,128)(2,1)} %copy-done.1, bf16[32,16384]{1,0:T(8,128)(2,1)} %collective-permute-done.refs_2_, bf16[32,16384]{1,0:T(8,128)(2,1)} %copy-done.2, bf16[16,16384]{1,0:T(8,128)(2,1)} %collective-permute-done.2.refs_4_, ...), custom_call_target="tpu_custom_call" | custom-call | flops 20000000000 | bytes 60000000 | tf_op jit(solution)/shard_map/update/pallas_call | solution.py:344
Async XLA Ops:
  0.0 12.3 %copy-start = (f32[32,16384]{1,0:T(8,128)S(1)}, f32[32,16384]{1,0:T(8,128)}, u32[]{:S(2)}) copy-start(f32[32,16384]{1,0:T(8,128)} %refs_7_.1) | copy-start | bytes 6291460
  2.8 22.5 %all-to-all-start = ((bf16[32,80,128]{2,1,0:T(8,128)(2,1)}), bf16[32,80,128]{2,1,0:T(8,128)(2,1)}, u32[]{:S(2)}, u32[]{:S(2)}) async-start(bf16[32,80,128]{2,1,0:T(8,128)(2,1)} %pack.1), calls=%async_computation | async-start | bytes 1310720 | tf_op jit(solution)/shard_map/all_to_all | solution.py:298
  12.5 4.8 %copy-start.1 = (bf16[32,16384]{1,0:T(8,128)(2,1)}, bf16[32,16384]{1,0:T(8,128)(2,1)S(1)}, u32[]{:S(2)}) copy-start(bf16[32,16384]{1,0:T(8,128)(2,1)S(1)} %convert_element_type.3.refs_1_) | copy-start | bytes 3145732
  12.5 27.7 %collective-permute-start.1 = (bf16[32,16384]{1,0:T(8,128)(2,1)S(1)}, bf16[32,16384]{1,0:T(8,128)(2,1)S(1)}, u32[]{:S(2)}, u32[]{:S(2)}) collective-permute-start(bf16[32,16384]{1,0:T(8,128)(2,1)S(1)} %convert_element_type.3.refs_1_), channel_id=1, source_target_pairs={{0,96},{32,0},{64,32},{96,64},{1,97},{33,1},{65,33},{97,65},{2,98}... | collective-permute-start | bytes 3145736 | tf_op jit(solution)/shard_map/ppermute | solution.py:287
  15.3 25.4 %collective-permute-start = (bf16[32,16384]{1,0:T(8,128)(2,1)S(1)}, bf16[32,16384]{1,0:T(8,128)(2,1)}, u32[]{:S(2)}, u32[]{:S(2)}) collective-permute-start(bf16[32,16384]{1,0:T(8,128)(2,1)S(1)} %convert_element_type.3.refs_1_), channel_id=1, source_target_pairs={{0,32},{32,64},{64,96},{96,0},{1,33},{33,65},{65,97},{97,1},{2,34}... | collective-permute-start | bytes 3145736 | tf_op jit(solution)/shard_map/ppermute | solution.py:287
  40.2 1.0 copy-start.2
  41.2 50.2 %all-to-all-start.1 = ((bf16[128,80,128]{2,1,0:T(8,128)(2,1)}), bf16[128,80,128]{2,1,0:T(8,128)(2,1)S(1)}, u32[]{:S(2)}, u32[]{:S(2)}) async-start(bf16[128,80,128]{2,1,0:T(8,128)(2,1)} %owner.1), calls=%async_computation.1 | async-start | bytes 5242880 | tf_op jit(solution)/shard_map/all_to_all | solution.py:338
  52.2 38.0 %collective-permute-start.3 = (bf16[16,16384]{1,0:T(8,128)(2,1)}, bf16[16,16384]{1,0:T(8,128)(2,1)}, u32[]{:S(2)}, u32[]{:S(2)}) collective-permute-start(bf16[16,16384]{1,0:T(8,128)(2,1)} %slice.7), channel_id=1, source_target_pairs={{0,96},{32,0},{64,32},{96,64},{1,97},{33,1},{65,33},{97,65},{2,98}... | collective-permute-start | bytes 1572872 | tf_op jit(solution)/shard_map/ppermute | solution.py:287
  54.9 36.6 %collective-permute-start.2 = (bf16[16,16384]{1,0:T(8,128)(2,1)S(1)}, bf16[16,16384]{1,0:T(8,128)(2,1)}, u32[]{:S(2)}, u32[]{:S(2)}) collective-permute-start(bf16[16,16384]{1,0:T(8,128)(2,1)S(1)} %slice.6), channel_id=1, source_target_pairs={{0,32},{32,64},{64,96},{96,0},{1,33},{33,65},{65,97},{97,1},{2,34}... | collective-permute-start | bytes 1572872 | tf_op jit(solution)/shard_map/ppermute | solution.py:287

commit v2 on v1

--- a/solution.py
+++ b/solution.py
@@ -104,7 +104,7 @@
             ],
             axis=0,
         )
-        turned = stack.T
+        turned = stack.astype(BF16).T
         lefts.append(
             jnp.concatenate(
                 [turned[j * soundings : (j + 1) * soundings, :] for j in range(per_lane)], axis=1
@@ -182,7 +182,7 @@
             )
             * scale
         )
-        gain = solved.T.astype(BF16)
+        gain = solved.astype(BF16).T
         rounded = anomalies[t].astype(BF16)
         which = lax.broadcasted_iota(jnp.int32, (LANES, LANES), 0) // gates
         right = jnp.concatenate(
@@ -198,32 +198,56 @@
                 ]
 
 
-def update_kernel(me_ref, *refs, unit, capacity, pieces):
-    parts = refs[:-9]
-    recv_ref, members_ref, out_ref, model_ref, taper_ref, turn_ref, tiles_ref, sems, last = refs[-9:]
-    ensemble = model_ref.shape[0]
-    block = members_ref.shape[0]
-    mems = ensemble // block
-    half = block // 2
-    sources = recv_ref.shape[0]
-    filled = capacity * block
+def assemble_kernel(me_ref, *refs):
+    parts = refs[:-2]
+    out_ref, sems = refs[-2:]
+    half = parts[0].shape[0]
+    mems = len(parts) // 2
     me = me_ref[0]
-    spots = [(0, 0, block), (1, 0, block), (3, 0, block), (2, 0, half), (2, half, half)]
-    copies = [pltpu.make_async_copy(members_ref, out_ref, sems.at[len(spots)])]
-    for n, (ref, (r, start, size)) in enumerate(zip(parts, spots)):
-        first = pl.multiple_of(((me - r) & (mems - 1)) * block + start, half)
-        copies.append(pltpu.make_async_copy(ref, model_ref.at[pl.ds(first, size), :], sems.at[n]))
+    copies = []
+    for n, ref in enumerate(parts):
+        first = ((me - n // 2) & (mems - 1)) * 2 * half + (n % 2) * half
+        first = pl.multiple_of(first, half)
+        copies.append(pltpu.make_async_copy(ref, out_ref.at[pl.ds(first, half), :], sems.at[n]))
     for copy in copies:
         copy.start()
+    for copy in copies:
+        copy.wait()
+
+
+def update_kernel(
+    model_hbm_ref,
+    recv_ref,
+    members_ref,
+    out_ref,
+    model_ref,
+    taper_ref,
+    turn_ref,
+    tiles_ref,
+    model_sem,
+    held_sem,
+    table_sem,
+    *,
+    unit,
+    capacity,
+    pieces,
+):
+    sources = recv_ref.shape[0]
+    block = members_ref.shape[0]
+    filled = capacity * block
+    model = pltpu.make_async_copy(model_hbm_ref, model_ref, model_sem)
+    held = pltpu.make_async_copy(members_ref, out_ref, held_sem)
+    model.start()
+    held.start()
     taper_ref[...] = recv_ref[:, filled:, :].astype(F32).reshape(sources * 8 * capacity, LANES)
     for c in range(capacity):
         numbers = taper_ref[pl.ds(8 * c + pieces, sources, stride=8 * capacity), :].T
         turn_ref[c] = numbers[:8, :].astype(jnp.int32)
-    table = pltpu.make_async_copy(turn_ref, tiles_ref, last)
+    table = pltpu.make_async_copy(turn_ref, tiles_ref, table_sem)
     table.start()
     table.wait()
-    for copy in copies:
-        copy.wait()
+    model.wait()
+    held.wait()
 
     def turn(i, _):
         items = []
@@ -298,8 +322,10 @@
     got = lax.all_to_all(packed, "brick", split_axis=0, concat_axis=0, tiled=True)
 
     held, _ = lax.optimization_barrier((members, packed))
-    model0 = held.astype(BF16)
-    model1, model3 = shifted(model0, 1), shifted(model0, -1)
+    half = members.shape[0] // 2
+    upper, lower = held[:half].astype(BF16), held[half:].astype(BF16)
+    upper1, lower3 = shifted(upper, 1), shifted(lower, -1)
+    lower1, upper3 = shifted(lower, 1), shifted(upper, -1)
 
     brick, _ = lax.optimization_barrier((brick, packed))
     taper_rows = pl.pallas_call(
@@ -331,33 +357,45 @@
         cost_estimate=cost(15),
         name="owner",
     )(brick, got, observed.T, noise_std.T, taper_rows)
-    weight_send, model1, model3 = lax.optimization_barrier((weight_send, model1, model3))
-    half = members.shape[0] // 2
-    upper2, lower2 = shifted(model1[:half], 1), shifted(model3[half:], -1)
-    blocks = (model0, model1, model3, upper2, lower2)
+    weight_send, upper1, lower1, upper3, lower3 = lax.optimization_barrier(
+        (weight_send, upper1, lower1, upper3, lower3)
+    )
+    upper2, lower2 = shifted(upper1, 1), shifted(lower3, -1)
+    halves = (upper, lower, upper1, lower1, upper2, lower2, upper3, lower3)
     weight_recv = lax.all_to_all(
         weight_send, ("mem", "brick"), split_axis=0, concat_axis=0, tiled=True
     )
     me = lax.axis_index("mem").astype(jnp.int32).reshape(1)
     hbm = pl.BlockSpec(memory_space=pl.ANY)
+    model_all = pl.pallas_call(
+        assemble_kernel,
+        out_shape=sds((ensemble, members.shape[1]), BF16),
+        in_specs=[smem()] + [hbm] * (2 * mems),
+        out_specs=vmem(1)[0],
+        scratch_shapes=[pltpu.SemaphoreType.DMA((2 * mems,))],
+        compiler_params=params(),
+        cost_estimate=cost(40),
+        name="assemble",
+    )(me, *halves)
     weight_recv = pltpu.with_memory_space_constraint(weight_recv, pltpu.VMEM)
     return pl.pallas_call(
         lambda *refs: update_kernel(*refs, unit=16, capacity=capacity, pieces=pieces),
         out_shape=sds(members.shape, F32),
-        in_specs=[smem()] + [hbm] * len(blocks) + vmem(1) + [hbm],
+        in_specs=[hbm] + vmem(1) + [hbm],
         out_specs=vmem(1)[0],
         scratch_shapes=[
-            pltpu.VMEM((ensemble, members.shape[1]), BF16),
+            pltpu.VMEM(model_all.shape, BF16),
             pltpu.VMEM((devices * 8 * capacity, LANES), F32),
             pltpu.VMEM((capacity, 8, devices), jnp.int32),
             pltpu.SMEM((capacity, 8, devices), jnp.int32),
-            pltpu.SemaphoreType.DMA((len(blocks) + 1,)),
+            pltpu.SemaphoreType.DMA(()),
+            pltpu.SemaphoreType.DMA(()),
             pltpu.SemaphoreType.DMA(()),
         ],
         compiler_params=params(),
         cost_estimate=cost(20),
         name="update",
-    )(me, *blocks, weight_recv, members)
+    )(model_all, weight_recv, members)
 
 
 def solution(mesh):

time: 108 us -> 105 us (0.972)
  waiting for transfers between devices: 45.1 us -> 37.1 us
  Pallas kernels: 36.2 us -> 40 us
  starting transfers between devices: 23 us -> 26 us
  local copies, waits for them, and re-layouts: 3.42 us -> 1.22 us
    ppermute x4 -> x6, waiting for transfers between devices: 37.1 us -> 3.23 us  [shifted(): return lax.ppermute(x, 'mem', [(i, (i + by) % mems) for i in range(mems)])]
    all_to_all x1, waiting for transfers between devices: 0.01 us -> 28.7 us  [body(): lax.all_to_all(weight_send, ('mem', 'brick'), split_axis=0, concat_axis=0...]
    pallas_call x0 -> x1, Pallas kernels: none -> 4.18 us  [body(): pl.pallas_call(assemble_kernel, out_shape=sds((ensemble, members.shape[1]...]
    slice x2 -> x1, local copies, waits for them, and re-layouts: 2.95 us -> 0.07 us  [body(): upper, lower = (held[:half].astype(BF16), held[half:].astype(BF16))]
    all_to_all x1, waiting for transfers between devices: 8.01 us -> 5.2 us  [body(): lax.all_to_all(packed, 'brick', split_axis=0, concat_axis=0, tiled=True)]
    ppermute x4 -> x6, starting transfers between devices: 5.46 us -> 8.26 us  [shifted(): return lax.ppermute(x, 'mem', [(i, (i + by) % mems) for i in range(mems)])]
  transfers between devices with their start and end apart: 6 -> 8, of which waited for: 4 -> 5; matrix products, arithmetic and copies ran while one was open for 3% -> 0% of each run, Pallas kernels for 16% -> 20%
where the time goes in v2:
time: 105 us
  Pallas kernels  40 us (38%)
  waiting for transfers between devices  37.1 us (35%)
  starting transfers between devices  26 us (25%)
  local copies, waits for them, and re-layouts  1.22 us (1%)
    all_to_all x1, waiting for transfers between devices, body(): lax.all_to_all(weight_send, ('mem', 'brick'), split_axis=0, concat_axis=0...  28.7 us
    pallas_call x1, Pallas kernels, body(): pl.pallas_call(lambda *refs: update_kernel(*refs, unit=16, capacity=capac...  16.6 us
    pallas_call x1, Pallas kernels, body(): pl.pallas_call(owner_kernel, out_shape=sds((devices, capacity * (ensemble...  14.5 us
    all_to_all x1, starting transfers between devices, body(): lax.all_to_all(packed, 'brick', split_axis=0, concat_axis=0, tiled=True)  9.43 us
    all_to_all x1, starting transfers between devices, body(): lax.all_to_all(weight_send, ('mem', 'brick'), split_axis=0, concat_axis=0...  8.27 us
    ppermute x6, starting transfers between devices, shifted(): return lax.ppermute(x, 'mem', [(i, (i + by) % mems) for i in range(mems)])  8.26 us
    all_to_all x1, waiting for transfers between devices, body(): lax.all_to_all(packed, 'brick', split_axis=0, concat_axis=0, tiled=True)  5.2 us
    pallas_call x1, Pallas kernels, body(): pl.pallas_call(assemble_kernel, out_shape=sds((ensemble, members.shape[1]...  4.18 us
  transfers between devices with their start and end apart: 8, of which 5 were waited for; matrix products, arithmetic and copies ran while one was open for 0% of the time, Pallas kernels for 20%

profile of v2, /device:TPU:1, one launch (start us, length us, event | category | flops | bytes accessed | tf_op | source)
XLA Modules:
  0.0 104.7 jit_solution(3220187697798891541)
XLA Ops:
  0.0 2.8 %pack.1 = bf16[32,80,128]{2,1,0:T(8,128)(2,1)} custom-call(f32[4,40,1024]{2,1,0:T(8,128)} %refs_0_.1, f32[4,40,1024]{2,1,0:T(8,128)} %refs_1_.1), custom_call_target="tpu_custom_call" | custom-call | flops 3000000000 | bytes 9000000 | tf_op jit(solution)/shard_map/pack/pallas_call | solution.py:313
  2.8 9.4 %all-to-all-start = ((bf16[32,80,128]{2,1,0:T(8,128)(2,1)}), bf16[32,80,128]{2,1,0:T(8,128)(2,1)S(1)}, u32[]{:S(2)}, u32[]{:S(2)}) async-start(bf16[32,80,128]{2,1,0:T(8,128)(2,1)} %pack.1), calls=%async_computation | async-start | bytes 1310720 | tf_op jit(solution)/shard_map/all_to_all | solution.py:322
  12.3 0.0 copy-done
  12.3 0.1 convert.4
  12.4 0.1 fusion
  12.5 0.0 copy-start.2
  12.5 0.0 copy-start.3
  12.5 2.8 %collective-permute-start.3 = (bf16[16,16384]{1,0:T(8,128)(2,1)S(1)}, bf16[16,16384]{1,0:T(8,128)(2,1)}, u32[]{:S(2)}, u32[]{:S(2)}) collective-permute-start(bf16[16,16384]{1,0:T(8,128)(2,1)S(1)} %get-tuple-element.19.refs_1_), channel_id=1, source_target_pairs={{0,96},{32,0},{64,32},{96,64},{1,97},{33,1},{65,33},{97,65},{2,98}... | collective-permute-start | bytes 1572872 | tf_op jit(solution)/shard_map/ppermute | solution.py:311
  15.3 0.0 collective-permute-start.1
  15.3 2.7 %collective-permute-start.2 = (bf16[16,16384]{1,0:T(8,128)(2,1)S(1)}, bf16[16,16384]{1,0:T(8,128)(2,1)S(1)}, u32[]{:S(2)}, u32[]{:S(2)}) collective-permute-start(bf16[16,16384]{1,0:T(8,128)(2,1)S(1)} %get-tuple-element.20.refs_0_), channel_id=1, source_target_pairs={{0,96},{32,0},{64,32},{96,64},{1,97},{33,1},{65,33},{97,65},{2,98}... | collective-permute-start | bytes 1572872 | tf_op jit(solution)/shard_map/ppermute | solution.py:311
  18.0 0.0 collective-permute-start
  18.0 2.0 %route_taper.1.taper_ref = bf16[32,16,128]{2,1,0:T(8,128)(2,1)} custom-call(s32[32]{0:T(128)} %bitcast.8, bf16[32,512]{1,0:T(8,128)(2,1)} %taper_ref.1, s32[4,32]{1,0:T(4,128)} %bitcast.7), custom_call_target="tpu_custom_call" | custom-call | flops 2000000000 | bytes 6000000 | tf_op jit(solution)/shard_map/route_taper/pallas_call | solution.py:331
  20.0 0.0 copy-done.2
  20.0 0.0 copy-done.3
  20.0 5.2 %all-to-all-done.got_ref = bf16[32,80,128]{2,1,0:T(8,128)(2,1)S(1)} async-done(((bf16[32,80,128]{2,1,0:T(8,128)(2,1)}), bf16[32,80,128]{2,1,0:T(8,128)(2,1)S(1)}, u32[]{:S(2)}, u32[]{:S(2)}) %all-to-all-start) | async-done | bytes 655392 | tf_op jit(solution)/shard_map/all_to_all | solution.py:322
  25.2 0.8 copy-done.1
  26.0 14.5 %owner.1 = bf16[128,80,128]{2,1,0:T(8,128)(2,1)} custom-call(s32[32]{0:T(128)} %bitcast.9, bf16[32,80,128]{2,1,0:T(8,128)(2,1)} %copy-done.1, f32[32,40]{1,0:T(8,128)} %bitcast.5, f32[32,40]{1,0:T(8,128)} %bitcast.6, bf16[32,16,128]{2,1,0:T(8,128)(2,1)} %route_taper.1.taper_ref), custom_call_target="tpu_custom_call" | custom-call | flops 15000000512 | bytes 45000000 | tf_op jit(solution)/shard_map/owner/pallas_call | solution.py:346
  40.5 0.0 collective-permute-done.3.refs_7_
  40.5 0.0 collective-permute-done.1.refs_3_
  40.5 0.0 copy-start.4
  40.5 0.0 collective-permute-done.2.refs_6_
  40.5 0.0 copy-start.5
  40.5 0.3 collective-permute-done.refs_2_
  40.8 1.1 %collective-permute-start.4 = (bf16[16,16384]{1,0:T(8,128)(2,1)}, bf16[16,16384]{1,0:T(8,128)(2,1)S(1)}, u32[]{:S(2)}, u32[]{:S(2)}) collective-permute-start(bf16[16,16384]{1,0:T(8,128)(2,1)} %collective-permute-done.refs_2_), channel_id=1, source_target_pairs={{0,32},{32,64},{64,96},{96,0},{1,33},{33,65},{65,97},{97,1},{2,34}... | collective-permute-start | bytes 1572872 | tf_op jit(solution)/shard_map/ppermute | solution.py:311
  41.9 1.7 %collective-permute-start.5 = (bf16[16,16384]{1,0:T(8,128)(2,1)}, bf16[16,16384]{1,0:T(8,128)(2,1)}, u32[]{:S(2)}, u32[]{:S(2)}) collective-permute-start(bf16[16,16384]{1,0:T(8,128)(2,1)} %collective-permute-done.3.refs_7_), channel_id=1, source_target_pairs={{0,96},{32,0},{64,32},{96,64},{1,97},{33,1},{65,33},{97,65},{2,98}... | collective-permute-start | bytes 1572872 | tf_op jit(solution)/shard_map/ppermute | solution.py:311
  43.6 8.3 %all-to-all-start.1 = ((bf16[128,80,128]{2,1,0:T(8,128)(2,1)}), bf16[128,80,128]{2,1,0:T(8,128)(2,1)S(1)}, u32[]{:S(2)}, u32[]{:S(2)}) async-start(bf16[128,80,128]{2,1,0:T(8,128)(2,1)} %owner.1), calls=%async_computation.1 | async-start | bytes 5242880 | tf_op jit(solution)/shard_map/all_to_all | solution.py:365
  51.9 2.4 %collective-permute-done.4.refs_4_ = bf16[16,16384]{1,0:T(8,128)(2,1)S(1)} collective-permute-done((bf16[16,16384]{1,0:T(8,128)(2,1)}, bf16[16,16384]{1,0:T(8,128)(2,1)S(1)}, u32[]{:S(2)}, u32[]{:S(2)}) %collective-permute-start.4) | collective-permute-done | bytes 524320 | tf_op jit(solution)/shard_map/ppermute | solution.py:311
  54.3 0.5 collective-permute-done.5.refs_5_
  54.8 0.3 copy-done.6
  55.1 4.2 %assemble.1.refs_0_ = bf16[128,16384]{1,0:T(8,128)(2,1)} custom-call(s32[1]{0:T(128)} %bitcast.me_ref, bf16[16,16384]{1,0:T(8,128)(2,1)} %copy-done.3, bf16[16,16384]{1,0:T(8,128)(2,1)} %copy-done.2, bf16[16,16384]{1,0:T(8,128)(2,1)} %collective-permute-done.refs_2_, bf16[16,16384]{1,0:T(8,128)(2,1)} %copy-done.4, bf16[16,16384]{1,0:T(8,128)(2,1)} %copy-done.6, ...), custom_call_target="tpu_custom_call" | custom-call | flops 40000000000 | bytes 120000000 | tf_op jit(solution)/shard_map/assemble/pallas_call | solution.py:370
  59.3 28.7 %all-to-all-done.1.refs_1_ = bf16[128,80,128]{2,1,0:T(8,128)(2,1)S(1)} async-done(((bf16[128,80,128]{2,1,0:T(8,128)(2,1)}), bf16[128,80,128]{2,1,0:T(8,128)(2,1)S(1)}, u32[]{:S(2)}, u32[]{:S(2)}) %all-to-all-start.1) | async-done | bytes 2621472 | tf_op jit(solution)/shard_map/all_to_all | solution.py:365
  88.0 16.6 %update.1 = f32[32,16384]{1,0:T(8,128)} custom-call(bf16[128,16384]{1,0:T(8,128)(2,1)} %assemble.1.refs_0_, bf16[128,80,128]{2,1,0:T(8,128)(2,1)S(1)} %all-to-all-done.1.refs_1_, f32[32,16384]{1,0:T(8,128)} %refs_2_.1), custom_call_target="tpu_custom_call" | custom-call | flops 20000000000 | bytes 60000000 | tf_op jit(solution)/shard_map/update/pallas_call | solution.py:381
  (5 shorter events, 0.0 us)
Async XLA Ops:
  0.0 12.3 %copy-start = (f32[32,16384]{1,0:T(8,128)S(1)}, f32[32,16384]{1,0:T(8,128)}, u32[]{:S(2)}) copy-start(f32[32,16384]{1,0:T(8,128)} %refs_2_.1) | copy-start | bytes 6291460
  2.8 22.3 %all-to-all-start = ((bf16[32,80,128]{2,1,0:T(8,128)(2,1)}), bf16[32,80,128]{2,1,0:T(8,128)(2,1)S(1)}, u32[]{:S(2)}, u32[]{:S(2)}) async-start(bf16[32,80,128]{2,1,0:T(8,128)(2,1)} %pack.1), calls=%async_computation | async-start | bytes 1310720 | tf_op jit(solution)/shard_map/all_to_all | solution.py:322
  12.5 7.5 %copy-start.2 = (bf16[16,16384]{1,0:T(8,128)(2,1)}, bf16[16,16384]{1,0:T(8,128)(2,1)S(1)}, u32[]{:S(2)}) copy-start(bf16[16,16384]{1,0:T(8,128)(2,1)S(1)} %get-tuple-element.19.refs_1_) | copy-start | bytes 1572868
  12.5 7.5 %copy-start.3 = (bf16[16,16384]{1,0:T(8,128)(2,1)}, bf16[16,16384]{1,0:T(8,128)(2,1)S(1)}, u32[]{:S(2)}) copy-start(bf16[16,16384]{1,0:T(8,128)(2,1)S(1)} %get-tuple-element.20.refs_0_) | copy-start | bytes 1572868
  12.5 28.0 %collective-permute-start.3 = (bf16[16,16384]{1,0:T(8,128)(2,1)S(1)}, bf16[16,16384]{1,0:T(8,128)(2,1)}, u32[]{:S(2)}, u32[]{:S(2)}) collective-permute-start(bf16[16,16384]{1,0:T(8,128)(2,1)S(1)} %get-tuple-element.19.refs_1_), channel_id=1, source_target_pairs={{0,96},{32,0},{64,32},{96,64},{1,97},{33,1},{65,33},{97,65},{2,98}... | collective-permute-start | bytes 1572872 | tf_op jit(solution)/shard_map/ppermute | solution.py:311
  15.3 25.2 %collective-permute-start.1 = (bf16[16,16384]{1,0:T(8,128)(2,1)S(1)}, bf16[16,16384]{1,0:T(8,128)(2,1)S(1)}, u32[]{:S(2)}, u32[]{:S(2)}) collective-permute-start(bf16[16,16384]{1,0:T(8,128)(2,1)S(1)} %get-tuple-element.19.refs_1_), channel_id=1, source_target_pairs={{0,32},{32,64},{64,96},{96,0},{1,33},{33,65},{65,97},{97,1},{2,34}... | collective-permute-start | bytes 1572872 | tf_op jit(solution)/shard_map/ppermute | solution.py:311
  15.3 25.2 %collective-permute-start.2 = (bf16[16,16384]{1,0:T(8,128)(2,1)S(1)}, bf16[16,16384]{1,0:T(8,128)(2,1)S(1)}, u32[]{:S(2)}, u32[]{:S(2)}) collective-permute-start(bf16[16,16384]{1,0:T(8,128)(2,1)S(1)} %get-tuple-element.20.refs_0_), channel_id=1, source_target_pairs={{0,96},{32,0},{64,32},{96,64},{1,97},{33,1},{65,33},{97,65},{2,98}... | collective-permute-start | bytes 1572872 | tf_op jit(solution)/shard_map/ppermute | solution.py:311
  18.0 22.8 %collective-permute-start = (bf16[16,16384]{1,0:T(8,128)(2,1)S(1)}, bf16[16,16384]{1,0:T(8,128)(2,1)}, u32[]{:S(2)}, u32[]{:S(2)}) collective-permute-start(bf16[16,16384]{1,0:T(8,128)(2,1)S(1)} %get-tuple-element.20.refs_0_), channel_id=1, source_target_pairs={{0,32},{32,64},{64,96},{96,0},{1,33},{33,65},{65,97},{97,1},{2,34}... | collective-permute-start | bytes 1572872 | tf_op jit(solution)/shard_map/ppermute | solution.py:311
  25.2 0.8 copy-start.1
  40.5 3.1 %copy-start.4 = (bf16[16,16384]{1,0:T(8,128)(2,1)}, bf16[16,16384]{1,0:T(8,128)(2,1)S(1)}, u32[]{:S(2)}) copy-start(bf16[16,16384]{1,0:T(8,128)(2,1)S(1)} %collective-permute-done.1.refs_3_) | copy-start | bytes 1572868
  40.5 3.1 %copy-start.5 = (bf16[16,16384]{1,0:T(8,128)(2,1)}, bf16[16,16384]{1,0:T(8,128)(2,1)S(1)}, u32[]{:S(2)}) copy-start(bf16[16,16384]{1,0:T(8,128)(2,1)S(1)} %collective-permute-done.2.refs_6_) | copy-start | bytes 1572868
  40.8 13.5 %collective-permute-start.4 = (bf16[16,16384]{1,0:T(8,128)(2,1)}, bf16[16,16384]{1,0:T(8,128)(2,1)S(1)}, u32[]{:S(2)}, u32[]{:S(2)}) collective-permute-start(bf16[16,16384]{1,0:T(8,128)(2,1)} %collective-permute-done.refs_2_), channel_id=1, source_target_pairs={{0,32},{32,64},{64,96},{96,0},{1,33},{33,65},{65,97},{97,1},{2,34}... | collective-permute-start | bytes 1572872 | tf_op jit(solution)/shard_map/ppermute | solution.py:311
  41.9 12.9 %collective-permute-start.5 = (bf16[16,16384]{1,0:T(8,128)(2,1)}, bf16[16,16384]{1,0:T(8,128)(2,1)}, u32[]{:S(2)}, u32[]{:S(2)}) collective-permute-start(bf16[16,16384]{1,0:T(8,128)(2,1)} %collective-permute-done.3.refs_7_), channel_id=1, source_target_pairs={{0,96},{32,0},{64,32},{96,64},{1,97},{33,1},{65,33},{97,65},{2,98}... | collective-permute-start | bytes 1572872 | tf_op jit(solution)/shard_map/ppermute | solution.py:311
  43.6 44.4 %all-to-all-start.1 = ((bf16[128,80,128]{2,1,0:T(8,128)(2,1)}), bf16[128,80,128]{2,1,0:T(8,128)(2,1)S(1)}, u32[]{:S(2)}, u32[]{:S(2)}) async-start(bf16[128,80,128]{2,1,0:T(8,128)(2,1)} %owner.1), calls=%async_computation.1 | async-start | bytes 5242880 | tf_op jit(solution)/shard_map/all_to_all | solution.py:365
  54.3 0.8 copy-start.6

commit v3 on v2

--- a/solution.py
+++ b/solution.py
@@ -343,6 +343,7 @@
         name="route_taper",
     )(brick, taper_weights, foot_tiles.T)
 
+    got = pltpu.with_memory_space_constraint(got, pltpu.VMEM)
     weight_send = pl.pallas_call(
         owner_kernel,
         out_shape=sds((devices, capacity * (ensemble // mems + 8), ensemble), BF16),

time: 105 us -> 105 us (level)
  transfers between devices with their start and end apart: 8 -> 8, of which waited for: 5 -> 4; matrix products, arithmetic and copies ran while one was open for 0% -> 0% of each run, Pallas kernels for 20% -> 20%
where the time goes in v3:
time: 105 us
  Pallas kernels  39.9 us (38%)
  waiting for transfers between devices  37.6 us (36%)
  starting transfers between devices  26 us (25%)
    all_to_all x1, waiting for transfers between devices, body(): lax.all_to_all(weight_send, ('mem', 'brick'), split_axis=0, concat_axis=0...  28.7 us
    pallas_call x1, Pallas kernels, body(): pl.pallas_call(lambda *refs: update_kernel(*refs, unit=16, capacity=capac...  16.6 us
    pallas_call x1, Pallas kernels, body(): pl.pallas_call(owner_kernel, out_shape=sds((devices, capacity * (ensemble...  14.3 us
    all_to_all x1, starting transfers between devices, body(): lax.all_to_all(packed, 'brick', split_axis=0, concat_axis=0, tiled=True)  9.43 us
    all_to_all x1, starting transfers between devices, body(): lax.all_to_all(weight_send, ('mem', 'brick'), split_axis=0, concat_axis=0...  8.38 us
    ppermute x6, starting transfers between devices, shifted(): return lax.ppermute(x, 'mem', [(i, (i + by) % mems) for i in range(mems)])  8.16 us
    all_to_all x1, waiting for transfers between devices, body(): lax.all_to_all(packed, 'brick', split_axis=0, concat_axis=0, tiled=True)  5.2 us
    pallas_call x1, Pallas kernels, body(): pl.pallas_call(assemble_kernel, out_shape=sds((ensemble, members.shape[1]...  4.18 us
  transfers between devices with their start and end apart: 8, of which 4 were waited for; matrix products, arithmetic and copies ran while one was open for 0% of the time, Pallas kernels for 20%

profile of v3, /device:TPU:1, one launch (start us, length us, event | category | flops | bytes accessed | tf_op | source)
XLA Modules:
  0.0 104.7 jit_solution(12244684258807921087)
XLA Ops:
  0.0 2.8 %pack.1 = bf16[32,80,128]{2,1,0:T(8,128)(2,1)} custom-call(f32[4,40,1024]{2,1,0:T(8,128)} %refs_0_.1, f32[4,40,1024]{2,1,0:T(8,128)} %refs_1_.1), custom_call_target="tpu_custom_call" | custom-call | flops 3000000000 | bytes 9000000 | tf_op jit(solution)/shard_map/pack/pallas_call | solution.py:313
  2.8 9.4 %all-to-all-start = ((bf16[32,80,128]{2,1,0:T(8,128)(2,1)}), bf16[32,80,128]{2,1,0:T(8,128)(2,1)S(1)}, u32[]{:S(2)}, u32[]{:S(2)}) async-start(bf16[32,80,128]{2,1,0:T(8,128)(2,1)} %pack.1), calls=%async_computation | async-start | bytes 1310720 | tf_op jit(solution)/shard_map/all_to_all | solution.py:322
  12.3 0.0 copy-done
  12.3 0.1 convert.4
  12.4 0.1 fusion
  12.5 0.0 copy-start.1
  12.5 0.0 copy-start.2
  12.5 2.8 %collective-permute-start.3 = (bf16[16,16384]{1,0:T(8,128)(2,1)S(1)}, bf16[16,16384]{1,0:T(8,128)(2,1)}, u32[]{:S(2)}, u32[]{:S(2)}) collective-permute-start(bf16[16,16384]{1,0:T(8,128)(2,1)S(1)} %get-tuple-element.19.refs_1_), channel_id=1, source_target_pairs={{0,96},{32,0},{64,32},{96,64},{1,97},{33,1},{65,33},{97,65},{2,98}... | collective-permute-start | bytes 1572872 | tf_op jit(solution)/shard_map/ppermute | solution.py:311
  15.3 0.0 collective-permute-start.1
  15.3 2.7 %collective-permute-start.2 = (bf16[16,16384]{1,0:T(8,128)(2,1)S(1)}, bf16[16,16384]{1,0:T(8,128)(2,1)S(1)}, u32[]{:S(2)}, u32[]{:S(2)}) collective-permute-start(bf16[16,16384]{1,0:T(8,128)(2,1)S(1)} %get-tuple-element.20.refs_0_), channel_id=1, source_target_pairs={{0,96},{32,0},{64,32},{96,64},{1,97},{33,1},{65,33},{97,65},{2,98}... | collective-permute-start | bytes 1572872 | tf_op jit(solution)/shard_map/ppermute | solution.py:311
  18.0 0.0 collective-permute-start
  18.0 2.0 %route_taper.1.taper_ref = bf16[32,16,128]{2,1,0:T(8,128)(2,1)} custom-call(s32[32]{0:T(128)} %bitcast.8, bf16[32,512]{1,0:T(8,128)(2,1)} %taper_ref.1, s32[4,32]{1,0:T(4,128)} %bitcast.7), custom_call_target="tpu_custom_call" | custom-call | flops 2000000000 | bytes 6000000 | tf_op jit(solution)/shard_map/route_taper/pallas_call | solution.py:331
  20.0 0.0 copy-done.1
  20.0 0.0 copy-done.2
  20.0 5.2 %all-to-all-done.got_ref = bf16[32,80,128]{2,1,0:T(8,128)(2,1)S(1)} async-done(((bf16[32,80,128]{2,1,0:T(8,128)(2,1)}), bf16[32,80,128]{2,1,0:T(8,128)(2,1)S(1)}, u32[]{:S(2)}, u32[]{:S(2)}) %all-to-all-start) | async-done | bytes 655392 | tf_op jit(solution)/shard_map/all_to_all | solution.py:322
  25.2 14.3 %owner.1 = bf16[128,80,128]{2,1,0:T(8,128)(2,1)} custom-call(s32[32]{0:T(128)} %bitcast.9, bf16[32,80,128]{2,1,0:T(8,128)(2,1)S(1)} %all-to-all-done.got_ref, f32[32,40]{1,0:T(8,128)} %bitcast.5, f32[32,40]{1,0:T(8,128)} %bitcast.6, bf16[32,16,128]{2,1,0:T(8,128)(2,1)} %route_taper.1.taper_ref), custom_call_target="tpu_custom_call" | custom-call | flops 15000000512 | bytes 45000000 | tf_op jit(solution)/shard_map/owner/pallas_call | solution.py:347
  39.5 0.0 collective-permute-done.3.refs_7_
  39.5 0.0 collective-permute-done.1.refs_3_
  39.5 0.0 collective-permute-done.2.refs_6_
  39.5 0.0 copy-start.4
  39.5 1.3 %collective-permute-done.refs_2_ = bf16[16,16384]{1,0:T(8,128)(2,1)} collective-permute-done((bf16[16,16384]{1,0:T(8,128)(2,1)S(1)}, bf16[16,16384]{1,0:T(8,128)(2,1)}, u32[]{:S(2)}, u32[]{:S(2)}) %collective-permute-start) | collective-permute-done | bytes 524320 | tf_op jit(solution)/shard_map/ppermute | solution.py:311
  40.8 0.0 collective-permute-start.4
  40.9 2.6 %collective-permute-start.5 = (bf16[16,16384]{1,0:T(8,128)(2,1)}, bf16[16,16384]{1,0:T(8,128)(2,1)}, u32[]{:S(2)}, u32[]{:S(2)}) collective-permute-start(bf16[16,16384]{1,0:T(8,128)(2,1)} %collective-permute-done.3.refs_7_), channel_id=1, source_target_pairs={{0,96},{32,0},{64,32},{96,64},{1,97},{33,1},{65,33},{97,65},{2,98}... | collective-permute-start | bytes 1572872 | tf_op jit(solution)/shard_map/ppermute | solution.py:311
  43.5 0.0 copy-done.3
  43.5 0.0 copy-done.4
  43.5 8.4 %all-to-all-start.1 = ((bf16[128,80,128]{2,1,0:T(8,128)(2,1)}), bf16[128,80,128]{2,1,0:T(8,128)(2,1)S(1)}, u32[]{:S(2)}, u32[]{:S(2)}) async-start(bf16[128,80,128]{2,1,0:T(8,128)(2,1)} %owner.1), calls=%async_computation.1 | async-start | bytes 5242880 | tf_op jit(solution)/shard_map/all_to_all | solution.py:366
  51.9 2.4 %collective-permute-done.4.refs_4_ = bf16[16,16384]{1,0:T(8,128)(2,1)S(1)} collective-permute-done((bf16[16,16384]{1,0:T(8,128)(2,1)}, bf16[16,16384]{1,0:T(8,128)(2,1)S(1)}, u32[]{:S(2)}, u32[]{:S(2)}) %collective-permute-start.4) | collective-permute-done | bytes 524320 | tf_op jit(solution)/shard_map/ppermute | solution.py:311
  54.3 0.0 collective-permute-done.5.refs_5_
  54.3 0.8 copy-done.5
  55.1 4.2 %assemble.1.refs_0_ = bf16[128,16384]{1,0:T(8,128)(2,1)} custom-call(s32[1]{0:T(128)} %bitcast.me_ref, bf16[16,16384]{1,0:T(8,128)(2,1)} %copy-done.2, bf16[16,16384]{1,0:T(8,128)(2,1)} %copy-done.1, bf16[16,16384]{1,0:T(8,128)(2,1)} %collective-permute-done.refs_2_, bf16[16,16384]{1,0:T(8,128)(2,1)} %copy-done.3, bf16[16,16384]{1,0:T(8,128)(2,1)} %copy-done.5, ...), custom_call_target="tpu_custom_call" | custom-call | flops 40000000000 | bytes 120000000 | tf_op jit(solution)/shard_map/assemble/pallas_call | solution.py:371
  59.3 28.7 %all-to-all-done.1.refs_1_ = bf16[128,80,128]{2,1,0:T(8,128)(2,1)S(1)} async-done(((bf16[128,80,128]{2,1,0:T(8,128)(2,1)}), bf16[128,80,128]{2,1,0:T(8,128)(2,1)S(1)}, u32[]{:S(2)}, u32[]{:S(2)}) %all-to-all-start.1) | async-done | bytes 2621472 | tf_op jit(solution)/shard_map/all_to_all | solution.py:366
  88.0 16.6 %update.1 = f32[32,16384]{1,0:T(8,128)} custom-call(bf16[128,16384]{1,0:T(8,128)(2,1)} %assemble.1.refs_0_, bf16[128,80,128]{2,1,0:T(8,128)(2,1)S(1)} %all-to-all-done.1.refs_1_, f32[32,16384]{1,0:T(8,128)} %refs_2_.1), custom_call_target="tpu_custom_call" | custom-call | flops 20000000000 | bytes 60000000 | tf_op jit(solution)/shard_map/update/pallas_call | solution.py:382
  (3 shorter events, 0.0 us)
Async XLA Ops:
  0.0 12.3 %copy-start = (f32[32,16384]{1,0:T(8,128)S(1)}, f32[32,16384]{1,0:T(8,128)}, u32[]{:S(2)}) copy-start(f32[32,16384]{1,0:T(8,128)} %refs_2_.1) | copy-start | bytes 6291460
  2.8 22.3 %all-to-all-start = ((bf16[32,80,128]{2,1,0:T(8,128)(2,1)}), bf16[32,80,128]{2,1,0:T(8,128)(2,1)S(1)}, u32[]{:S(2)}, u32[]{:S(2)}) async-start(bf16[32,80,128]{2,1,0:T(8,128)(2,1)} %pack.1), calls=%async_computation | async-start | bytes 1310720 | tf_op jit(solution)/shard_map/all_to_all | solution.py:322
  12.5 7.5 %copy-start.1 = (bf16[16,16384]{1,0:T(8,128)(2,1)}, bf16[16,16384]{1,0:T(8,128)(2,1)S(1)}, u32[]{:S(2)}) copy-start(bf16[16,16384]{1,0:T(8,128)(2,1)S(1)} %get-tuple-element.19.refs_1_) | copy-start | bytes 1572868
  12.5 7.5 %copy-start.2 = (bf16[16,16384]{1,0:T(8,128)(2,1)}, bf16[16,16384]{1,0:T(8,128)(2,1)S(1)}, u32[]{:S(2)}) copy-start(bf16[16,16384]{1,0:T(8,128)(2,1)S(1)} %get-tuple-element.20.refs_0_) | copy-start | bytes 1572868
  12.5 27.0 %collective-permute-start.3 = (bf16[16,16384]{1,0:T(8,128)(2,1)S(1)}, bf16[16,16384]{1,0:T(8,128)(2,1)}, u32[]{:S(2)}, u32[]{:S(2)}) collective-permute-start(bf16[16,16384]{1,0:T(8,128)(2,1)S(1)} %get-tuple-element.19.refs_1_), channel_id=1, source_target_pairs={{0,96},{32,0},{64,32},{96,64},{1,97},{33,1},{65,33},{97,65},{2,98}... | collective-permute-start | bytes 1572872 | tf_op jit(solution)/shard_map/ppermute | solution.py:311
  15.3 24.2 %collective-permute-start.1 = (bf16[16,16384]{1,0:T(8,128)(2,1)S(1)}, bf16[16,16384]{1,0:T(8,128)(2,1)S(1)}, u32[]{:S(2)}, u32[]{:S(2)}) collective-permute-start(bf16[16,16384]{1,0:T(8,128)(2,1)S(1)} %get-tuple-element.19.refs_1_), channel_id=1, source_target_pairs={{0,32},{32,64},{64,96},{96,0},{1,33},{33,65},{65,97},{97,1},{2,34}... | collective-permute-start | bytes 1572872 | tf_op jit(solution)/shard_map/ppermute | solution.py:311
  15.3 24.2 %collective-permute-start.2 = (bf16[16,16384]{1,0:T(8,128)(2,1)S(1)}, bf16[16,16384]{1,0:T(8,128)(2,1)S(1)}, u32[]{:S(2)}, u32[]{:S(2)}) collective-permute-start(bf16[16,16384]{1,0:T(8,128)(2,1)S(1)} %get-tuple-element.20.refs_0_), channel_id=1, source_target_pairs={{0,96},{32,0},{64,32},{96,64},{1,97},{33,1},{65,33},{97,65},{2,98}... | collective-permute-start | bytes 1572872 | tf_op jit(solution)/shard_map/ppermute | solution.py:311
  18.0 22.8 %collective-permute-start = (bf16[16,16384]{1,0:T(8,128)(2,1)S(1)}, bf16[16,16384]{1,0:T(8,128)(2,1)}, u32[]{:S(2)}, u32[]{:S(2)}) collective-permute-start(bf16[16,16384]{1,0:T(8,128)(2,1)S(1)} %get-tuple-element.20.refs_0_), channel_id=1, source_target_pairs={{0,32},{32,64},{64,96},{96,0},{1,33},{33,65},{65,97},{97,1},{2,34}... | collective-permute-start | bytes 1572872 | tf_op jit(solution)/shard_map/ppermute | solution.py:311
  39.5 4.0 %copy-start.3 = (bf16[16,16384]{1,0:T(8,128)(2,1)}, bf16[16,16384]{1,0:T(8,128)(2,1)S(1)}, u32[]{:S(2)}) copy-start(bf16[16,16384]{1,0:T(8,128)(2,1)S(1)} %collective-permute-done.1.refs_3_) | copy-start | bytes 1572868
  39.5 4.0 %copy-start.4 = (bf16[16,16384]{1,0:T(8,128)(2,1)}, bf16[16,16384]{1,0:T(8,128)(2,1)S(1)}, u32[]{:S(2)}) copy-start(bf16[16,16384]{1,0:T(8,128)(2,1)S(1)} %collective-permute-done.2.refs_6_) | copy-start | bytes 1572868
  40.8 13.5 %collective-permute-start.4 = (bf16[16,16384]{1,0:T(8,128)(2,1)}, bf16[16,16384]{1,0:T(8,128)(2,1)S(1)}, u32[]{:S(2)}, u32[]{:S(2)}) collective-permute-start(bf16[16,16384]{1,0:T(8,128)(2,1)} %collective-permute-done.refs_2_), channel_id=1, source_target_pairs={{0,32},{32,64},{64,96},{96,0},{1,33},{33,65},{65,97},{97,1},{2,34}... | collective-permute-start | bytes 1572872 | tf_op jit(solution)/shard_map/ppermute | solution.py:311
  40.9 13.4 %collective-permute-start.5 = (bf16[16,16384]{1,0:T(8,128)(2,1)}, bf16[16,16384]{1,0:T(8,128)(2,1)}, u32[]{:S(2)}, u32[]{:S(2)}) collective-permute-start(bf16[16,16384]{1,0:T(8,128)(2,1)} %collective-permute-done.3.refs_7_), channel_id=1, source_target_pairs={{0,96},{32,0},{64,32},{96,64},{1,97},{33,1},{65,33},{97,65},{2,98}... | collective-permute-start | bytes 1572872 | tf_op jit(solution)/shard_map/ppermute | solution.py:311
  43.5 44.5 %all-to-all-start.1 = ((bf16[128,80,128]{2,1,0:T(8,128)(2,1)}), bf16[128,80,128]{2,1,0:T(8,128)(2,1)S(1)}, u32[]{:S(2)}, u32[]{:S(2)}) async-start(bf16[128,80,128]{2,1,0:T(8,128)(2,1)} %owner.1), calls=%async_computation.1 | async-start | bytes 5242880 | tf_op jit(solution)/shard_map/all_to_all | solution.py:366
  54.3 0.8 copy-start.5

commit v4 on v3

--- a/solution.py
+++ b/solution.py
@@ -380,7 +380,7 @@
     )(me, *halves)
     weight_recv = pltpu.with_memory_space_constraint(weight_recv, pltpu.VMEM)
     return pl.pallas_call(
-        lambda *refs: update_kernel(*refs, unit=16, capacity=capacity, pieces=pieces),
+        lambda *refs: update_kernel(*refs, unit=32, capacity=capacity, pieces=pieces),
         out_shape=sds(members.shape, F32),
         in_specs=[hbm] + vmem(1) + [hbm],
         out_specs=vmem(1)[0],

time: 105 us -> 104 us (level)
  no operation moved by 1% of the time
where the time goes in v4:
time: 104 us
  Pallas kernels  39.2 us (38%)
  waiting for transfers between devices  37.6 us (36%)
  starting transfers between devices  26 us (25%)
    all_to_all x1, waiting for transfers between devices, body(): lax.all_to_all(weight_send, ('mem', 'brick'), split_axis=0, concat_axis=0...  28.7 us
    pallas_call x1, Pallas kernels, body(): pl.pallas_call(lambda *refs: update_kernel(*refs, unit=32, capacity=capac...  15.9 us
    pallas_call x1, Pallas kernels, body(): pl.pallas_call(owner_kernel, out_shape=sds((devices, capacity * (ensemble...  14.3 us
    all_to_all x1, starting transfers between devices, body(): lax.all_to_all(packed, 'brick', split_axis=0, concat_axis=0, tiled=True)  9.43 us
    all_to_all x1, starting transfers between devices, body(): lax.all_to_all(weight_send, ('mem', 'brick'), split_axis=0, concat_axis=0...  8.38 us
    ppermute x6, starting transfers between devices, shifted(): return lax.ppermute(x, 'mem', [(i, (i + by) % mems) for i in range(mems)])  8.16 us
    all_to_all x1, waiting for transfers between devices, body(): lax.all_to_all(packed, 'brick', split_axis=0, concat_axis=0, tiled=True)  5.2 us
    pallas_call x1, Pallas kernels, body(): pl.pallas_call(assemble_kernel, out_shape=sds((ensemble, members.shape[1]...  4.18 us
  transfers between devices with their start and end apart: 8, of which 4 were waited for; matrix products, arithmetic and copies ran while one was open for 0% of the time, Pallas kernels for 20%

profile of v4, /device:TPU:1, one launch (start us, length us, event | category | flops | bytes accessed | tf_op | source)
XLA Modules:
  0.0 104.0 jit_solution(16336989149425649640)
XLA Ops:
  0.0 2.8 %pack.1 = bf16[32,80,128]{2,1,0:T(8,128)(2,1)} custom-call(f32[4,40,1024]{2,1,0:T(8,128)} %refs_0_.1, f32[4,40,1024]{2,1,0:T(8,128)} %refs_1_.1), custom_call_target="tpu_custom_call" | custom-call | flops 3000000000 | bytes 9000000 | tf_op jit(solution)/shard_map/pack/pallas_call | solution.py:313
  2.8 9.4 %all-to-all-start = ((bf16[32,80,128]{2,1,0:T(8,128)(2,1)}), bf16[32,80,128]{2,1,0:T(8,128)(2,1)S(1)}, u32[]{:S(2)}, u32[]{:S(2)}) async-start(bf16[32,80,128]{2,1,0:T(8,128)(2,1)} %pack.1), calls=%async_computation | async-start | bytes 1310720 | tf_op jit(solution)/shard_map/all_to_all | solution.py:322
  12.3 0.0 copy-done
  12.3 0.1 convert.4
  12.4 0.1 fusion
  12.5 0.0 copy-start.1
  12.5 0.0 copy-start.2
  12.5 2.8 %collective-permute-start.3 = (bf16[16,16384]{1,0:T(8,128)(2,1)S(1)}, bf16[16,16384]{1,0:T(8,128)(2,1)}, u32[]{:S(2)}, u32[]{:S(2)}) collective-permute-start(bf16[16,16384]{1,0:T(8,128)(2,1)S(1)} %get-tuple-element.19.refs_1_), channel_id=1, source_target_pairs={{0,96},{32,0},{64,32},{96,64},{1,97},{33,1},{65,33},{97,65},{2,98}... | collective-permute-start | bytes 1572872 | tf_op jit(solution)/shard_map/ppermute | solution.py:311
  15.3 0.0 collective-permute-start.1
  15.3 2.7 %collective-permute-start.2 = (bf16[16,16384]{1,0:T(8,128)(2,1)S(1)}, bf16[16,16384]{1,0:T(8,128)(2,1)S(1)}, u32[]{:S(2)}, u32[]{:S(2)}) collective-permute-start(bf16[16,16384]{1,0:T(8,128)(2,1)S(1)} %get-tuple-element.20.refs_0_), channel_id=1, source_target_pairs={{0,96},{32,0},{64,32},{96,64},{1,97},{33,1},{65,33},{97,65},{2,98}... | collective-permute-start | bytes 1572872 | tf_op jit(solution)/shard_map/ppermute | solution.py:311
  18.0 0.0 collective-permute-start
  18.0 2.0 %route_taper.1.taper_ref = bf16[32,16,128]{2,1,0:T(8,128)(2,1)} custom-call(s32[32]{0:T(128)} %bitcast.8, bf16[32,512]{1,0:T(8,128)(2,1)} %taper_ref.1, s32[4,32]{1,0:T(4,128)} %bitcast.7), custom_call_target="tpu_custom_call" | custom-call | flops 2000000000 | bytes 6000000 | tf_op jit(solution)/shard_map/route_taper/pallas_call | solution.py:331
  20.0 0.0 copy-done.1
  20.0 0.0 copy-done.2
  20.0 5.2 %all-to-all-done.got_ref = bf16[32,80,128]{2,1,0:T(8,128)(2,1)S(1)} async-done(((bf16[32,80,128]{2,1,0:T(8,128)(2,1)}), bf16[32,80,128]{2,1,0:T(8,128)(2,1)S(1)}, u32[]{:S(2)}, u32[]{:S(2)}) %all-to-all-start) | async-done | bytes 655392 | tf_op jit(solution)/shard_map/all_to_all | solution.py:322
  25.2 14.3 %owner.1 = bf16[128,80,128]{2,1,0:T(8,128)(2,1)} custom-call(s32[32]{0:T(128)} %bitcast.9, bf16[32,80,128]{2,1,0:T(8,128)(2,1)S(1)} %all-to-all-done.got_ref, f32[32,40]{1,0:T(8,128)} %bitcast.5, f32[32,40]{1,0:T(8,128)} %bitcast.6, bf16[32,16,128]{2,1,0:T(8,128)(2,1)} %route_taper.1.taper_ref), custom_call_target="tpu_custom_call" | custom-call | flops 15000000512 | bytes 45000000 | tf_op jit(solution)/shard_map/owner/pallas_call | solution.py:347
  39.5 0.0 collective-permute-done.3.refs_7_
  39.5 0.0 collective-permute-done.1.refs_3_
  39.5 0.0 collective-permute-done.2.refs_6_
  39.5 0.0 copy-start.4
  39.5 1.3 %collective-permute-done.refs_2_ = bf16[16,16384]{1,0:T(8,128)(2,1)} collective-permute-done((bf16[16,16384]{1,0:T(8,128)(2,1)S(1)}, bf16[16,16384]{1,0:T(8,128)(2,1)}, u32[]{:S(2)}, u32[]{:S(2)}) %collective-permute-start) | collective-permute-done | bytes 524320 | tf_op jit(solution)/shard_map/ppermute | solution.py:311
  40.8 0.0 collective-permute-start.4
  40.9 2.6 %collective-permute-start.5 = (bf16[16,16384]{1,0:T(8,128)(2,1)}, bf16[16,16384]{1,0:T(8,128)(2,1)}, u32[]{:S(2)}, u32[]{:S(2)}) collective-permute-start(bf16[16,16384]{1,0:T(8,128)(2,1)} %collective-permute-done.3.refs_7_), channel_id=1, source_target_pairs={{0,96},{32,0},{64,32},{96,64},{1,97},{33,1},{65,33},{97,65},{2,98}... | collective-permute-start | bytes 1572872 | tf_op jit(solution)/shard_map/ppermute | solution.py:311
  43.5 0.0 copy-done.3
  43.5 0.0 copy-done.4
  43.5 8.4 %all-to-all-start.1 = ((bf16[128,80,128]{2,1,0:T(8,128)(2,1)}), bf16[128,80,128]{2,1,0:T(8,128)(2,1)S(1)}, u32[]{:S(2)}, u32[]{:S(2)}) async-start(bf16[128,80,128]{2,1,0:T(8,128)(2,1)} %owner.1), calls=%async_computation.1 | async-start | bytes 5242880 | tf_op jit(solution)/shard_map/all_to_all | solution.py:366
  51.9 2.4 %collective-permute-done.4.refs_4_ = bf16[16,16384]{1,0:T(8,128)(2,1)S(1)} collective-permute-done((bf16[16,16384]{1,0:T(8,128)(2,1)}, bf16[16,16384]{1,0:T(8,128)(2,1)S(1)}, u32[]{:S(2)}, u32[]{:S(2)}) %collective-permute-start.4) | collective-permute-done | bytes 524320 | tf_op jit(solution)/shard_map/ppermute | solution.py:311
  54.3 0.0 collective-permute-done.5.refs_5_
  54.3 0.8 copy-done.5
  55.1 4.2 %assemble.1.refs_0_ = bf16[128,16384]{1,0:T(8,128)(2,1)} custom-call(s32[1]{0:T(128)} %bitcast.me_ref, bf16[16,16384]{1,0:T(8,128)(2,1)} %copy-done.2, bf16[16,16384]{1,0:T(8,128)(2,1)} %copy-done.1, bf16[16,16384]{1,0:T(8,128)(2,1)} %collective-permute-done.refs_2_, bf16[16,16384]{1,0:T(8,128)(2,1)} %copy-done.3, bf16[16,16384]{1,0:T(8,128)(2,1)} %copy-done.5, ...), custom_call_target="tpu_custom_call" | custom-call | flops 40000000000 | bytes 120000000 | tf_op jit(solution)/shard_map/assemble/pallas_call | solution.py:371
  59.3 28.7 %all-to-all-done.1.refs_1_ = bf16[128,80,128]{2,1,0:T(8,128)(2,1)S(1)} async-done(((bf16[128,80,128]{2,1,0:T(8,128)(2,1)}), bf16[128,80,128]{2,1,0:T(8,128)(2,1)S(1)}, u32[]{:S(2)}, u32[]{:S(2)}) %all-to-all-start.1) | async-done | bytes 2621472 | tf_op jit(solution)/shard_map/all_to_all | solution.py:366
  88.0 15.9 %update.1 = f32[32,16384]{1,0:T(8,128)} custom-call(bf16[128,16384]{1,0:T(8,128)(2,1)} %assemble.1.refs_0_, bf16[128,80,128]{2,1,0:T(8,128)(2,1)S(1)} %all-to-all-done.1.refs_1_, f32[32,16384]{1,0:T(8,128)} %refs_2_.1), custom_call_target="tpu_custom_call" | custom-call | flops 20000000000 | bytes 60000000 | tf_op jit(solution)/shard_map/update/pallas_call | solution.py:382
  (3 shorter events, 0.0 us)
Async XLA Ops:
  0.0 12.3 %copy-start = (f32[32,16384]{1,0:T(8,128)S(1)}, f32[32,16384]{1,0:T(8,128)}, u32[]{:S(2)}) copy-start(f32[32,16384]{1,0:T(8,128)} %refs_2_.1) | copy-start | bytes 6291460
  2.8 22.3 %all-to-all-start = ((bf16[32,80,128]{2,1,0:T(8,128)(2,1)}), bf16[32,80,128]{2,1,0:T(8,128)(2,1)S(1)}, u32[]{:S(2)}, u32[]{:S(2)}) async-start(bf16[32,80,128]{2,1,0:T(8,128)(2,1)} %pack.1), calls=%async_computation | async-start | bytes 1310720 | tf_op jit(solution)/shard_map/all_to_all | solution.py:322
  12.5 7.5 %copy-start.1 = (bf16[16,16384]{1,0:T(8,128)(2,1)}, bf16[16,16384]{1,0:T(8,128)(2,1)S(1)}, u32[]{:S(2)}) copy-start(bf16[16,16384]{1,0:T(8,128)(2,1)S(1)} %get-tuple-element.19.refs_1_) | copy-start | bytes 1572868
  12.5 7.5 %copy-start.2 = (bf16[16,16384]{1,0:T(8,128)(2,1)}, bf16[16,16384]{1,0:T(8,128)(2,1)S(1)}, u32[]{:S(2)}) copy-start(bf16[16,16384]{1,0:T(8,128)(2,1)S(1)} %get-tuple-element.20.refs_0_) | copy-start | bytes 1572868
  12.5 27.0 %collective-permute-start.3 = (bf16[16,16384]{1,0:T(8,128)(2,1)S(1)}, bf16[16,16384]{1,0:T(8,128)(2,1)}, u32[]{:S(2)}, u32[]{:S(2)}) collective-permute-start(bf16[16,16384]{1,0:T(8,128)(2,1)S(1)} %get-tuple-element.19.refs_1_), channel_id=1, source_target_pairs={{0,96},{32,0},{64,32},{96,64},{1,97},{33,1},{65,33},{97,65},{2,98}... | collective-permute-start | bytes 1572872 | tf_op jit(solution)/shard_map/ppermute | solution.py:311
  15.3 24.2 %collective-permute-start.1 = (bf16[16,16384]{1,0:T(8,128)(2,1)S(1)}, bf16[16,16384]{1,0:T(8,128)(2,1)S(1)}, u32[]{:S(2)}, u32[]{:S(2)}) collective-permute-start(bf16[16,16384]{1,0:T(8,128)(2,1)S(1)} %get-tuple-element.19.refs_1_), channel_id=1, source_target_pairs={{0,32},{32,64},{64,96},{96,0},{1,33},{33,65},{65,97},{97,1},{2,34}... | collective-permute-start | bytes 1572872 | tf_op jit(solution)/shard_map/ppermute | solution.py:311
  15.3 24.2 %collective-permute-start.2 = (bf16[16,16384]{1,0:T(8,128)(2,1)S(1)}, bf16[16,16384]{1,0:T(8,128)(2,1)S(1)}, u32[]{:S(2)}, u32[]{:S(2)}) collective-permute-start(bf16[16,16384]{1,0:T(8,128)(2,1)S(1)} %get-tuple-element.20.refs_0_), channel_id=1, source_target_pairs={{0,96},{32,0},{64,32},{96,64},{1,97},{33,1},{65,33},{97,65},{2,98}... | collective-permute-start | bytes 1572872 | tf_op jit(solution)/shard_map/ppermute | solution.py:311
  18.0 22.8 %collective-permute-start = (bf16[16,16384]{1,0:T(8,128)(2,1)S(1)}, bf16[16,16384]{1,0:T(8,128)(2,1)}, u32[]{:S(2)}, u32[]{:S(2)}) collective-permute-start(bf16[16,16384]{1,0:T(8,128)(2,1)S(1)} %get-tuple-element.20.refs_0_), channel_id=1, source_target_pairs={{0,32},{32,64},{64,96},{96,0},{1,33},{33,65},{65,97},{97,1},{2,34}... | collective-permute-start | bytes 1572872 | tf_op jit(solution)/shard_map/ppermute | solution.py:311
  39.5 4.0 %copy-start.3 = (bf16[16,16384]{1,0:T(8,128)(2,1)}, bf16[16,16384]{1,0:T(8,128)(2,1)S(1)}, u32[]{:S(2)}) copy-start(bf16[16,16384]{1,0:T(8,128)(2,1)S(1)} %collective-permute-done.1.refs_3_) | copy-start | bytes 1572868
  39.5 4.0 %copy-start.4 = (bf16[16,16384]{1,0:T(8,128)(2,1)}, bf16[16,16384]{1,0:T(8,128)(2,1)S(1)}, u32[]{:S(2)}) copy-start(bf16[16,16384]{1,0:T(8,128)(2,1)S(1)} %collective-permute-done.2.refs_6_) | copy-start | bytes 1572868
  40.8 13.5 %collective-permute-start.4 = (bf16[16,16384]{1,0:T(8,128)(2,1)}, bf16[16,16384]{1,0:T(8,128)(2,1)S(1)}, u32[]{:S(2)}, u32[]{:S(2)}) collective-permute-start(bf16[16,16384]{1,0:T(8,128)(2,1)} %collective-permute-done.refs_2_), channel_id=1, source_target_pairs={{0,32},{32,64},{64,96},{96,0},{1,33},{33,65},{65,97},{97,1},{2,34}... | collective-permute-start | bytes 1572872 | tf_op jit(solution)/shard_map/ppermute | solution.py:311
  40.9 13.4 %collective-permute-start.5 = (bf16[16,16384]{1,0:T(8,128)(2,1)}, bf16[16,16384]{1,0:T(8,128)(2,1)}, u32[]{:S(2)}, u32[]{:S(2)}) collective-permute-start(bf16[16,16384]{1,0:T(8,128)(2,1)} %collective-permute-done.3.refs_7_), channel_id=1, source_target_pairs={{0,96},{32,0},{64,32},{96,64},{1,97},{33,1},{65,33},{97,65},{2,98}... | collective-permute-start | bytes 1572872 | tf_op jit(solution)/shard_map/ppermute | solution.py:311
  43.5 44.5 %all-to-all-start.1 = ((bf16[128,80,128]{2,1,0:T(8,128)(2,1)}), bf16[128,80,128]{2,1,0:T(8,128)(2,1)S(1)}, u32[]{:S(2)}, u32[]{:S(2)}) async-start(bf16[128,80,128]{2,1,0:T(8,128)(2,1)} %owner.1), calls=%async_computation.1 | async-start | bytes 5242880 | tf_op jit(solution)/shard_map/all_to_all | solution.py:366
  54.3 0.8 copy-start.5
